TPU v7x, 256 devices: a whole 4x4x8 slice. The times are simulated.
256 devices in a mesh: elev: 16 (over z, core), valley: 8 (over x_lo, y), down: 2 (over x_hi).
Axes of the slice: x: 4 (x_hi: 2, x_lo: 2; x = x_hi * 2 + x_lo), y: 4, z: 8, core: 2. Of those that a mesh axis runs over, the one named last changes fastest.
Arguments:
- resid: bfloat16 [16, 32, 4, 128, 256], P('elev', 'valley', 'down'), may hold values from -6 to 6
- direction: bfloat16 [16, 32, 4, 128, 256], P('elev', 'valley', 'down'), may hold values from -6 to 6
- diag_blocks: bfloat16 [16, 32, 4, 256, 256], P('elev', 'valley', 'down'), may hold values from -0.375 to 0.375
- lower_blocks: bfloat16 [16, 32, 4, 256, 256], P('elev', 'valley', 'down')
- upper_blocks: bfloat16 [16, 32, 4, 256, 256], P('elev', 'valley', 'down')
- inv_pivots: bfloat16 [16, 32, 4, 256, 256], P('elev', 'valley', 'down')
- down_coupling: bfloat16 [16, 32, 4, 256, 256], P('elev', 'valley', 'down'), may hold values from -0.375 to 0.375
- valley_coupling: bfloat16 [16, 32, 4, 256, 256], P('elev', 'valley', 'down'), may hold values from -0.375 to 0.375
- coupled_column: int32 [16, 32, 4], P('elev', 'valley', 'down'), may hold values from 0 to 31
Outputs:
- preconditioned: bfloat16 [16, 32, 4, 128, 256], P('elev', 'valley', 'down')
- image: float32 [16, 32, 4, 128, 256], P('elev', 'valley', 'down')
All inputs are finite; a program needn't handle non-finite values.
Results may differ from a plain program's by a relative error of at most 0.015.
Values may be sent and summed in bfloat16 or wider, within the bound.
A program may use at most 64 MiB of HBM per device.

v0:
```python
import jax
import jax.numpy as jnp
from jax import lax
from jax.sharding import PartitionSpec as P


def from_behind(value, axis, by):
    length = lax.axis_size(axis)
    pairs = [(i, i + by) for i in range(length) if 0 <= i + by < length]
    return lax.ppermute(value, axis, pairs)


def with_halo(block, sides, width):
    for axis, dim in sides:
        count = lax.axis_size(axis)
        forward = [(i, i + 1) for i in range(count - 1)]
        backward = [(target, source) for source, target in forward]
        low = lax.ppermute(
            lax.slice_in_dim(block, block.shape[dim] - width, None, axis=dim), axis, forward
        )
        high = lax.ppermute(lax.slice_in_dim(block, 0, width, axis=dim), axis, backward)
        block = jnp.concatenate([low, block, high], axis=dim)
    return block


def apply_blocks(vectors, blocks):
    return jnp.einsum("bqrs,bqst->bqrt", vectors, blocks, preferred_element_type=jnp.float32)


def local(
    resid,
    direction,
    diag_blocks,
    lower_blocks,
    upper_blocks,
    inv_pivots,
    down_coupling,
    valley_coupling,
    coupled_column,
):
    rhs_local = resid[0]
    lower_local = lower_blocks[0]
    upper_local = upper_blocks[0]
    pivot_local = inv_pivots[0]
    valley_count = rhs_local.shape[0]
    chain_length = lax.axis_size("elev")
    height = lax.axis_index("elev")
    group_count = 1
    span_blocks = valley_count // group_count
    group_shape = (span_blocks,) + rhs_local.shape[1:]

    def forward_step(step, carry):
        incoming, store = carry
        group = step - height
        active = jnp.logical_and(group >= 0, group < group_count)
        chosen = jnp.clip(group, 0, group_count - 1)

        def forward_advance(operands):
            arriving, kept, which = operands
            inner = (rhs_local.astype(jnp.float32) - apply_blocks(arriving, lower_local)).astype(
                jnp.bfloat16
            )
            result = apply_blocks(inner, pivot_local).astype(jnp.bfloat16)
            return (result, result)

        def forward_remain(operands):
            arriving, kept, which = operands
            return (jnp.zeros_like(arriving), kept)

        result, store = lax.cond(active, forward_advance, forward_remain, (incoming, store, chosen))
        incoming = from_behind(result, "elev", 1)
        return (incoming, store)

    start_front = jnp.zeros(group_shape, jnp.bfloat16)
    _, fronts = lax.fori_loop(
        0, chain_length + group_count - 1, forward_step, (start_front, jnp.zeros_like(rhs_local))
    )
    depth = chain_length - 1 - height

    def backward_step(step, carry):
        incoming, store = carry
        group = step - depth
        active = jnp.logical_and(group >= 0, group < group_count)
        chosen = jnp.clip(group, 0, group_count - 1)

        def backward_advance(operands):
            arriving, kept, which = operands
            carried = apply_blocks(arriving, upper_local).astype(jnp.bfloat16)
            result = (fronts.astype(jnp.float32) - apply_blocks(carried, pivot_local)).astype(
                jnp.bfloat16
            )
            return (result, result)

        def backward_remain(operands):
            arriving, kept, which = operands
            return (jnp.zeros_like(arriving), kept)

        result, store = lax.cond(
            active, backward_advance, backward_remain, (incoming, store, chosen)
        )
        incoming = from_behind(result, "elev", -1)
        return (incoming, store)

    _, solved = lax.fori_loop(
        0, chain_length + group_count - 1, backward_step, (start_front, jnp.zeros_like(rhs_local))
    )
    current = direction[0]
    padded = with_halo(direction, (("elev", 0),), 1)
    below_dir = padded[0]
    above_dir = padded[2]
    rim_blocks = from_behind(current[:, -1:], "down", 1)
    upstream = jnp.concatenate([rim_blocks, current[:, :-1]], axis=1)
    partner_index = coupled_column[0]
    piece = lax.all_gather(current, "valley", axis=0, tiled=True)
    count = piece.shape[0]
    columns = jnp.arange(count, dtype=jnp.int32)
    picker = (partner_index[:, :, None] == columns[None, None, :]).astype(jnp.bfloat16)
    partner_sum = jnp.einsum("pqc,cqrs->pqrs", picker, piece, preferred_element_type=jnp.float32)
    partner = partner_sum.astype(jnp.bfloat16)
    total = apply_blocks(current, diag_blocks[0])
    total = total + apply_blocks(below_dir, lower_local)
    total = total + apply_blocks(above_dir, upper_local)
    total = total + apply_blocks(upstream, down_coupling[0])
    total = total + apply_blocks(partner, valley_coupling[0])
    return (solved[None], total[None])


def solution(mesh):
    in_specs = (
        P("elev", "valley", "down", None, None),
        P("elev", "valley", "down", None, None),
        P("elev", "valley", "down", None, None),
        P("elev", "valley", "down", None, None),
        P("elev", "valley", "down", None, None),
        P("elev", "valley", "down", None, None),
        P("elev", "valley", "down", None, None),
        P("elev", "valley", "down", None, None),
        P("elev", "valley", "down"),
    )
    out_specs = (P("elev", "valley", "down", None, None), P("elev", "valley", "down", None, None))
    return jax.shard_map(local, mesh=mesh, in_specs=in_specs, out_specs=out_specs, check_vma=False)
```

profile of v0, /device:TPU:97, one launch (start us, length us, event | category | flops | bytes accessed | tf_op | source)
XLA Modules:
  0.0 504.1 jit_solution(5448251669165728107)
XLA Ops:
  7.9 2.6 collective-permute-start.3
  10.5 4.7 collective-permute-start.2
  17.0 5.4 %collective-permute-start.4 = (bf16[4,1,128,256]{3,2,1,0:T(8,128)(2,1)}, bf16[4,1,128,256]{3,2,1,0:T(8,128)(2,1)}, u32[]{:S(2)}, u32[]{:S(2)}) collective-permute-start(bf16[4,1,128,256]{3,2,1,0:T(8,128)(2,1)} %get-tuple-element.314), channel_id=1, source_target_pairs={{0,1},{2,3},{4,5},{6,7},{8,9},{10,11},{12,13},{14,15},{16,17},{18,... | collective-permute-start | bytes 786440 | tf_op jit(solution)/shard_map/ppermute | solution.py:10
  23.9 7.3 %collective-permute-done.4 = bf16[4,1,128,256]{3,2,1,0:T(8,128)(2,1)} collective-permute-done((bf16[4,1,128,256]{3,2,1,0:T(8,128)(2,1)}, bf16[4,1,128,256]{3,2,1,0:T(8,128)(2,1)}, u32[]{:S(2)}, u32[]{:S(2)}) %collective-permute-start.4) | collective-permute-done | bytes 262176 | tf_op jit(solution)/shard_map/ppermute | solution.py:10
  31.2 2.6 fusion.10
  33.8 2.3 convolution_add_fusion.1
  36.2 33.4 %all-gather.3.cloned.1.call-done = bf16[1,32,2,128,256]{4,3,2,0,1:T(8,128)(2,1)} async-done(((bf16[1,4,2,128,256]{4,3,2,0,1:T(8,128)(2,1)}), bf16[1,32,2,128,256]{4,3,2,0,1:T(8,128)(2,1)}) %all-gather.3.cloned.1.call-update) | async-done | bytes 4194320 | tf_op jit(solution)/shard_map/all_gather | solution.py:114
  69.6 4.8 fusion.3
  76.0 2.5 fusion.7
  80.1 208.6 %while.36 = (s32[]{:T(128)}, bf16[4,2,128,256]{3,2,1,0:T(8,128)(2,1)}, bf16[4,2,128,256]{3,2,1,0:T(8,128)(2,1)}, s32[]{:T(128)}, bf16[4,2,128,256]{3,2,1,0:T(8,1...) while((s32[]{:T(128)}, ...), condition=%wide.region_3.0_spmd, body=%wide.region_0.0_spmd.sunk | while | flops 269484032 | bytes 6815963 | solution.py:75
  81.0 5.1 %collective-permute-start = (bf16[4,2,128,256]{3,2,1,0:T(8,128)(2,1)}, bf16[4,2,128,256]{3,2,1,0:T(8,128)(2,1)}, u32[]{:S(2)}, u32[]{:S(2)}) collective-permute-start(bf16[4,2,128,256]{3,2,1,0:T(8,128)(2,1)} %get-tuple-element.399), channel_id=1, source_target_pairs={{0,16},{16,32},{32,48},{48,64},{64,80},{80,96},{96,112},{112,128},... | collective-permute-start | bytes 1572872 | tf_op jit(solution)/shard_map/while/body/eval_jaxpr/ppermute | solution.py:10
  86.1 6.4 %collective-permute-done = bf16[4,2,128,256]{3,2,1,0:T(8,128)(2,1)} collective-permute-done((bf16[4,2,128,256]{3,2,1,0:T(8,128)(2,1)}, bf16[4,2,128,256]{3,2,1,0:T(8,128)(2,1)}, u32[]{:S(2)}, u32[]{:S(2)}) %collective-permute-start) | collective-permute-done | bytes 524320 | tf_op jit(solution)/shard_map/while/body/eval_jaxpr/ppermute | solution.py:10
  93.3 5.6 %collective-permute-start = (bf16[4,2,128,256]{3,2,1,0:T(8,128)(2,1)}, bf16[4,2,128,256]{3,2,1,0:T(8,128)(2,1)}, u32[]{:S(2)}, u32[]{:S(2)}) collective-permute-start(bf16[4,2,128,256]{3,2,1,0:T(8,128)(2,1)} %get-tuple-element.399), channel_id=1, source_target_pairs={{0,16},{16,32},{32,48},{48,64},{64,80},{80,96},{96,112},{112,128},... | collective-permute-start | bytes 1572872 | tf_op jit(solution)/shard_map/while/body/eval_jaxpr/ppermute | solution.py:10
  98.9 6.4 %collective-permute-done = bf16[4,2,128,256]{3,2,1,0:T(8,128)(2,1)} collective-permute-done((bf16[4,2,128,256]{3,2,1,0:T(8,128)(2,1)}, bf16[4,2,128,256]{3,2,1,0:T(8,128)(2,1)}, u32[]{:S(2)}, u32[]{:S(2)}) %collective-permute-start) | collective-permute-done | bytes 524320 | tf_op jit(solution)/shard_map/while/body/eval_jaxpr/ppermute | solution.py:10
  106.2 5.6 %collective-permute-start = (bf16[4,2,128,256]{3,2,1,0:T(8,128)(2,1)}, bf16[4,2,128,256]{3,2,1,0:T(8,128)(2,1)}, u32[]{:S(2)}, u32[]{:S(2)}) collective-permute-start(bf16[4,2,128,256]{3,2,1,0:T(8,128)(2,1)} %get-tuple-element.399), channel_id=1, source_target_pairs={{0,16},{16,32},{32,48},{48,64},{64,80},{80,96},{96,112},{112,128},... | collective-permute-start | bytes 1572872 | tf_op jit(solution)/shard_map/while/body/eval_jaxpr/ppermute | solution.py:10
  111.8 6.4 %collective-permute-done = bf16[4,2,128,256]{3,2,1,0:T(8,128)(2,1)} collective-permute-done((bf16[4,2,128,256]{3,2,1,0:T(8,128)(2,1)}, bf16[4,2,128,256]{3,2,1,0:T(8,128)(2,1)}, u32[]{:S(2)}, u32[]{:S(2)}) %collective-permute-start) | collective-permute-done | bytes 524320 | tf_op jit(solution)/shard_map/while/body/eval_jaxpr/ppermute | solution.py:10
  119.0 5.6 %collective-permute-start = (bf16[4,2,128,256]{3,2,1,0:T(8,128)(2,1)}, bf16[4,2,128,256]{3,2,1,0:T(8,128)(2,1)}, u32[]{:S(2)}, u32[]{:S(2)}) collective-permute-start(bf16[4,2,128,256]{3,2,1,0:T(8,128)(2,1)} %get-tuple-element.399), channel_id=1, source_target_pairs={{0,16},{16,32},{32,48},{48,64},{64,80},{80,96},{96,112},{112,128},... | collective-permute-start | bytes 1572872 | tf_op jit(solution)/shard_map/while/body/eval_jaxpr/ppermute | solution.py:10
  124.6 6.4 %collective-permute-done = bf16[4,2,128,256]{3,2,1,0:T(8,128)(2,1)} collective-permute-done((bf16[4,2,128,256]{3,2,1,0:T(8,128)(2,1)}, bf16[4,2,128,256]{3,2,1,0:T(8,128)(2,1)}, u32[]{:S(2)}, u32[]{:S(2)}) %collective-permute-start) | collective-permute-done | bytes 524320 | tf_op jit(solution)/shard_map/while/body/eval_jaxpr/ppermute | solution.py:10
  131.9 5.6 %collective-permute-start = (bf16[4,2,128,256]{3,2,1,0:T(8,128)(2,1)}, bf16[4,2,128,256]{3,2,1,0:T(8,128)(2,1)}, u32[]{:S(2)}, u32[]{:S(2)}) collective-permute-start(bf16[4,2,128,256]{3,2,1,0:T(8,128)(2,1)} %get-tuple-element.399), channel_id=1, source_target_pairs={{0,16},{16,32},{32,48},{48,64},{64,80},{80,96},{96,112},{112,128},... | collective-permute-start | bytes 1572872 | tf_op jit(solution)/shard_map/while/body/eval_jaxpr/ppermute | solution.py:10
  137.5 6.4 %collective-permute-done = bf16[4,2,128,256]{3,2,1,0:T(8,128)(2,1)} collective-permute-done((bf16[4,2,128,256]{3,2,1,0:T(8,128)(2,1)}, bf16[4,2,128,256]{3,2,1,0:T(8,128)(2,1)}, u32[]{:S(2)}, u32[]{:S(2)}) %collective-permute-start) | collective-permute-done | bytes 524320 | tf_op jit(solution)/shard_map/while/body/eval_jaxpr/ppermute | solution.py:10
  144.7 5.6 %collective-permute-start = (bf16[4,2,128,256]{3,2,1,0:T(8,128)(2,1)}, bf16[4,2,128,256]{3,2,1,0:T(8,128)(2,1)}, u32[]{:S(2)}, u32[]{:S(2)}) collective-permute-start(bf16[4,2,128,256]{3,2,1,0:T(8,128)(2,1)} %get-tuple-element.399), channel_id=1, source_target_pairs={{0,16},{16,32},{32,48},{48,64},{64,80},{80,96},{96,112},{112,128},... | collective-permute-start | bytes 1572872 | tf_op jit(solution)/shard_map/while/body/eval_jaxpr/ppermute | solution.py:10
  150.3 6.4 %collective-permute-done = bf16[4,2,128,256]{3,2,1,0:T(8,128)(2,1)} collective-permute-done((bf16[4,2,128,256]{3,2,1,0:T(8,128)(2,1)}, bf16[4,2,128,256]{3,2,1,0:T(8,128)(2,1)}, u32[]{:S(2)}, u32[]{:S(2)}) %collective-permute-start) | collective-permute-done | bytes 524320 | tf_op jit(solution)/shard_map/while/body/eval_jaxpr/ppermute | solution.py:10
  157.6 5.6 %collective-permute-start = (bf16[4,2,128,256]{3,2,1,0:T(8,128)(2,1)}, bf16[4,2,128,256]{3,2,1,0:T(8,128)(2,1)}, u32[]{:S(2)}, u32[]{:S(2)}) collective-permute-start(bf16[4,2,128,256]{3,2,1,0:T(8,128)(2,1)} %get-tuple-element.399), channel_id=1, source_target_pairs={{0,16},{16,32},{32,48},{48,64},{64,80},{80,96},{96,112},{112,128},... | collective-permute-start | bytes 1572872 | tf_op jit(solution)/shard_map/while/body/eval_jaxpr/ppermute | solution.py:10
  163.2 6.4 %collective-permute-done = bf16[4,2,128,256]{3,2,1,0:T(8,128)(2,1)} collective-permute-done((bf16[4,2,128,256]{3,2,1,0:T(8,128)(2,1)}, bf16[4,2,128,256]{3,2,1,0:T(8,128)(2,1)}, u32[]{:S(2)}, u32[]{:S(2)}) %collective-permute-start) | collective-permute-done | bytes 524320 | tf_op jit(solution)/shard_map/while/body/eval_jaxpr/ppermute | solution.py:10
  169.6 4.3 conditional.4
  169.6 2.5 convolution_convert_fusion
  173.9 2.1 collective-permute-start
  176.0 6.4 %collective-permute-done = bf16[4,2,128,256]{3,2,1,0:T(8,128)(2,1)} collective-permute-done((bf16[4,2,128,256]{3,2,1,0:T(8,128)(2,1)}, bf16[4,2,128,256]{3,2,1,0:T(8,128)(2,1)}, u32[]{:S(2)}, u32[]{:S(2)}) %collective-permute-start) | collective-permute-done | bytes 524320 | tf_op jit(solution)/shard_map/while/body/eval_jaxpr/ppermute | solution.py:10
  183.3 9.1 %collective-permute-start = (bf16[4,2,128,256]{3,2,1,0:T(8,128)(2,1)}, bf16[4,2,128,256]{3,2,1,0:T(8,128)(2,1)}, u32[]{:S(2)}, u32[]{:S(2)}) collective-permute-start(bf16[4,2,128,256]{3,2,1,0:T(8,128)(2,1)} %get-tuple-element.399), channel_id=1, source_target_pairs={{0,16},{16,32},{32,48},{48,64},{64,80},{80,96},{96,112},{112,128},... | collective-permute-start | bytes 1572872 | tf_op jit(solution)/shard_map/while/body/eval_jaxpr/ppermute | solution.py:10
  192.4 6.4 %collective-permute-done = bf16[4,2,128,256]{3,2,1,0:T(8,128)(2,1)} collective-permute-done((bf16[4,2,128,256]{3,2,1,0:T(8,128)(2,1)}, bf16[4,2,128,256]{3,2,1,0:T(8,128)(2,1)}, u32[]{:S(2)}, u32[]{:S(2)}) %collective-permute-start) | collective-permute-done | bytes 524320 | tf_op jit(solution)/shard_map/while/body/eval_jaxpr/ppermute | solution.py:10
  199.6 5.6 %collective-permute-start = (bf16[4,2,128,256]{3,2,1,0:T(8,128)(2,1)}, bf16[4,2,128,256]{3,2,1,0:T(8,128)(2,1)}, u32[]{:S(2)}, u32[]{:S(2)}) collective-permute-start(bf16[4,2,128,256]{3,2,1,0:T(8,128)(2,1)} %get-tuple-element.399), channel_id=1, source_target_pairs={{0,16},{16,32},{32,48},{48,64},{64,80},{80,96},{96,112},{112,128},... | collective-permute-start | bytes 1572872 | tf_op jit(solution)/shard_map/while/body/eval_jaxpr/ppermute | solution.py:10
  205.2 6.4 %collective-permute-done = bf16[4,2,128,256]{3,2,1,0:T(8,128)(2,1)} collective-permute-done((bf16[4,2,128,256]{3,2,1,0:T(8,128)(2,1)}, bf16[4,2,128,256]{3,2,1,0:T(8,128)(2,1)}, u32[]{:S(2)}, u32[]{:S(2)}) %collective-permute-start) | collective-permute-done | bytes 524320 | tf_op jit(solution)/shard_map/while/body/eval_jaxpr/ppermute | solution.py:10
  212.5 5.6 %collective-permute-start = (bf16[4,2,128,256]{3,2,1,0:T(8,128)(2,1)}, bf16[4,2,128,256]{3,2,1,0:T(8,128)(2,1)}, u32[]{:S(2)}, u32[]{:S(2)}) collective-permute-start(bf16[4,2,128,256]{3,2,1,0:T(8,128)(2,1)} %get-tuple-element.399), channel_id=1, source_target_pairs={{0,16},{16,32},{32,48},{48,64},{64,80},{80,96},{96,112},{112,128},... | collective-permute-start | bytes 1572872 | tf_op jit(solution)/shard_map/while/body/eval_jaxpr/ppermute | solution.py:10
  218.1 6.4 %collective-permute-done = bf16[4,2,128,256]{3,2,1,0:T(8,128)(2,1)} collective-permute-done((bf16[4,2,128,256]{3,2,1,0:T(8,128)(2,1)}, bf16[4,2,128,256]{3,2,1,0:T(8,128)(2,1)}, u32[]{:S(2)}, u32[]{:S(2)}) %collective-permute-start) | collective-permute-done | bytes 524320 | tf_op jit(solution)/shard_map/while/body/eval_jaxpr/ppermute | solution.py:10
  225.3 5.6 %collective-permute-start = (bf16[4,2,128,256]{3,2,1,0:T(8,128)(2,1)}, bf16[4,2,128,256]{3,2,1,0:T(8,128)(2,1)}, u32[]{:S(2)}, u32[]{:S(2)}) collective-permute-start(bf16[4,2,128,256]{3,2,1,0:T(8,128)(2,1)} %get-tuple-element.399), channel_id=1, source_target_pairs={{0,16},{16,32},{32,48},{48,64},{64,80},{80,96},{96,112},{112,128},... | collective-permute-start | bytes 1572872 | tf_op jit(solution)/shard_map/while/body/eval_jaxpr/ppermute | solution.py:10
  230.9 6.4 %collective-permute-done = bf16[4,2,128,256]{3,2,1,0:T(8,128)(2,1)} collective-permute-done((bf16[4,2,128,256]{3,2,1,0:T(8,128)(2,1)}, bf16[4,2,128,256]{3,2,1,0:T(8,128)(2,1)}, u32[]{:S(2)}, u32[]{:S(2)}) %collective-permute-start) | collective-permute-done | bytes 524320 | tf_op jit(solution)/shard_map/while/body/eval_jaxpr/ppermute | solution.py:10
  238.2 5.6 %collective-permute-start = (bf16[4,2,128,256]{3,2,1,0:T(8,128)(2,1)}, bf16[4,2,128,256]{3,2,1,0:T(8,128)(2,1)}, u32[]{:S(2)}, u32[]{:S(2)}) collective-permute-start(bf16[4,2,128,256]{3,2,1,0:T(8,128)(2,1)} %get-tuple-element.399), channel_id=1, source_target_pairs={{0,16},{16,32},{32,48},{48,64},{64,80},{80,96},{96,112},{112,128},... | collective-permute-start | bytes 1572872 | tf_op jit(solution)/shard_map/while/body/eval_jaxpr/ppermute | solution.py:10
  243.8 6.4 %collective-permute-done = bf16[4,2,128,256]{3,2,1,0:T(8,128)(2,1)} collective-permute-done((bf16[4,2,128,256]{3,2,1,0:T(8,128)(2,1)}, bf16[4,2,128,256]{3,2,1,0:T(8,128)(2,1)}, u32[]{:S(2)}, u32[]{:S(2)}) %collective-permute-start) | collective-permute-done | bytes 524320 | tf_op jit(solution)/shard_map/while/body/eval_jaxpr/ppermute | solution.py:10
  251.0 5.6 %collective-permute-start = (bf16[4,2,128,256]{3,2,1,0:T(8,128)(2,1)}, bf16[4,2,128,256]{3,2,1,0:T(8,128)(2,1)}, u32[]{:S(2)}, u32[]{:S(2)}) collective-permute-start(bf16[4,2,128,256]{3,2,1,0:T(8,128)(2,1)} %get-tuple-element.399), channel_id=1, source_target_pairs={{0,16},{16,32},{32,48},{48,64},{64,80},{80,96},{96,112},{112,128},... | collective-permute-start | bytes 1572872 | tf_op jit(solution)/shard_map/while/body/eval_jaxpr/ppermute | solution.py:10
  256.6 6.4 %collective-permute-done = bf16[4,2,128,256]{3,2,1,0:T(8,128)(2,1)} collective-permute-done((bf16[4,2,128,256]{3,2,1,0:T(8,128)(2,1)}, bf16[4,2,128,256]{3,2,1,0:T(8,128)(2,1)}, u32[]{:S(2)}, u32[]{:S(2)}) %collective-permute-start) | collective-permute-done | bytes 524320 | tf_op jit(solution)/shard_map/while/body/eval_jaxpr/ppermute | solution.py:10
  263.9 5.6 %collective-permute-start = (bf16[4,2,128,256]{3,2,1,0:T(8,128)(2,1)}, bf16[4,2,128,256]{3,2,1,0:T(8,128)(2,1)}, u32[]{:S(2)}, u32[]{:S(2)}) collective-permute-start(bf16[4,2,128,256]{3,2,1,0:T(8,128)(2,1)} %get-tuple-element.399), channel_id=1, source_target_pairs={{0,16},{16,32},{32,48},{48,64},{64,80},{80,96},{96,112},{112,128},... | collective-permute-start | bytes 1572872 | tf_op jit(solution)/shard_map/while/body/eval_jaxpr/ppermute | solution.py:10
  269.5 6.4 %collective-permute-done = bf16[4,2,128,256]{3,2,1,0:T(8,128)(2,1)} collective-permute-done((bf16[4,2,128,256]{3,2,1,0:T(8,128)(2,1)}, bf16[4,2,128,256]{3,2,1,0:T(8,128)(2,1)}, u32[]{:S(2)}, u32[]{:S(2)}) %collective-permute-start) | collective-permute-done | bytes 524320 | tf_op jit(solution)/shard_map/while/body/eval_jaxpr/ppermute | solution.py:10
  276.7 5.6 %collective-permute-start = (bf16[4,2,128,256]{3,2,1,0:T(8,128)(2,1)}, bf16[4,2,128,256]{3,2,1,0:T(8,128)(2,1)}, u32[]{:S(2)}, u32[]{:S(2)}) collective-permute-start(bf16[4,2,128,256]{3,2,1,0:T(8,128)(2,1)} %get-tuple-element.399), channel_id=1, source_target_pairs={{0,16},{16,32},{32,48},{48,64},{64,80},{80,96},{96,112},{112,128},... | collective-permute-start | bytes 1572872 | tf_op jit(solution)/shard_map/while/body/eval_jaxpr/ppermute | solution.py:10
  282.3 6.4 %collective-permute-done = bf16[4,2,128,256]{3,2,1,0:T(8,128)(2,1)} collective-permute-done((bf16[4,2,128,256]{3,2,1,0:T(8,128)(2,1)}, bf16[4,2,128,256]{3,2,1,0:T(8,128)(2,1)}, u32[]{:S(2)}, u32[]{:S(2)}) %collective-permute-start) | collective-permute-done | bytes 524320 | tf_op jit(solution)/shard_map/while/body/eval_jaxpr/ppermute | solution.py:10
  288.8 207.7 %while.37 = (s32[]{:T(128)}, bf16[4,2,128,256]{3,2,1,0:T(8,128)(2,1)S(1)}, bf16[4,2,128,256]{3,2,1,0:T(8,128)(2,1)S(1)}, s32[]{:T(128)}, bf16[4,2,128,256]{3,2,1...) while((s32[]{:T(128)}, ...), condition=%wide.region_7.0_spmd, body=%wide.region_4.0_spmd.sunk | while | flops 269484032 | bytes 6815963 | solution.py:104
  291.6 10.7 %collective-permute-done.1 = bf16[4,2,128,256]{3,2,1,0:T(8,128)(2,1)S(1)} collective-permute-done((bf16[4,2,128,256]{3,2,1,0:T(8,128)(2,1)}, bf16[4,2,128,256]{3,2,1,0:T(8,128)(2,1)S(1)}, u32[]{:S(2)}, u32[]{:S(2)}) %collective-permute-start.1) | collective-permute-done | bytes 524320 | tf_op jit(solution)/shard_map/while/body/eval_jaxpr/ppermute | solution.py:10
  303.2 1.9 collective-permute-start.1
  305.1 10.0 %collective-permute-done.1 = bf16[4,2,128,256]{3,2,1,0:T(8,128)(2,1)S(1)} collective-permute-done((bf16[4,2,128,256]{3,2,1,0:T(8,128)(2,1)}, bf16[4,2,128,256]{3,2,1,0:T(8,128)(2,1)S(1)}, u32[]{:S(2)}, u32[]{:S(2)}) %collective-permute-start.1) | collective-permute-done | bytes 524320 | tf_op jit(solution)/shard_map/while/body/eval_jaxpr/ppermute | solution.py:10
  317.9 10.0 %collective-permute-done.1 = bf16[4,2,128,256]{3,2,1,0:T(8,128)(2,1)S(1)} collective-permute-done((bf16[4,2,128,256]{3,2,1,0:T(8,128)(2,1)}, bf16[4,2,128,256]{3,2,1,0:T(8,128)(2,1)S(1)}, u32[]{:S(2)}, u32[]{:S(2)}) %collective-permute-start.1) | collective-permute-done | bytes 524320 | tf_op jit(solution)/shard_map/while/body/eval_jaxpr/ppermute | solution.py:10
  330.6 10.0 %collective-permute-done.1 = bf16[4,2,128,256]{3,2,1,0:T(8,128)(2,1)S(1)} collective-permute-done((bf16[4,2,128,256]{3,2,1,0:T(8,128)(2,1)}, bf16[4,2,128,256]{3,2,1,0:T(8,128)(2,1)S(1)}, u32[]{:S(2)}, u32[]{:S(2)}) %collective-permute-start.1) | collective-permute-done | bytes 524320 | tf_op jit(solution)/shard_map/while/body/eval_jaxpr/ppermute | solution.py:10
  343.4 10.0 %collective-permute-done.1 = bf16[4,2,128,256]{3,2,1,0:T(8,128)(2,1)S(1)} collective-permute-done((bf16[4,2,128,256]{3,2,1,0:T(8,128)(2,1)}, bf16[4,2,128,256]{3,2,1,0:T(8,128)(2,1)S(1)}, u32[]{:S(2)}, u32[]{:S(2)}) %collective-permute-start.1) | collective-permute-done | bytes 524320 | tf_op jit(solution)/shard_map/while/body/eval_jaxpr/ppermute | solution.py:10
  356.2 10.0 %collective-permute-done.1 = bf16[4,2,128,256]{3,2,1,0:T(8,128)(2,1)S(1)} collective-permute-done((bf16[4,2,128,256]{3,2,1,0:T(8,128)(2,1)}, bf16[4,2,128,256]{3,2,1,0:T(8,128)(2,1)S(1)}, u32[]{:S(2)}, u32[]{:S(2)}) %collective-permute-start.1) | collective-permute-done | bytes 524320 | tf_op jit(solution)/shard_map/while/body/eval_jaxpr/ppermute | solution.py:10
  368.9 10.0 %collective-permute-done.1 = bf16[4,2,128,256]{3,2,1,0:T(8,128)(2,1)S(1)} collective-permute-done((bf16[4,2,128,256]{3,2,1,0:T(8,128)(2,1)}, bf16[4,2,128,256]{3,2,1,0:T(8,128)(2,1)S(1)}, u32[]{:S(2)}, u32[]{:S(2)}) %collective-permute-start.1) | collective-permute-done | bytes 524320 | tf_op jit(solution)/shard_map/while/body/eval_jaxpr/ppermute | solution.py:10
  381.7 10.0 %collective-permute-done.1 = bf16[4,2,128,256]{3,2,1,0:T(8,128)(2,1)S(1)} collective-permute-done((bf16[4,2,128,256]{3,2,1,0:T(8,128)(2,1)}, bf16[4,2,128,256]{3,2,1,0:T(8,128)(2,1)S(1)}, u32[]{:S(2)}, u32[]{:S(2)}) %collective-permute-start.1) | collective-permute-done | bytes 524320 | tf_op jit(solution)/shard_map/while/body/eval_jaxpr/ppermute | solution.py:10
  391.7 3.7 conditional.5
  391.7 2.6 fusion.2
  397.2 10.0 %collective-permute-done.1 = bf16[4,2,128,256]{3,2,1,0:T(8,128)(2,1)S(1)} collective-permute-done((bf16[4,2,128,256]{3,2,1,0:T(8,128)(2,1)}, bf16[4,2,128,256]{3,2,1,0:T(8,128)(2,1)S(1)}, u32[]{:S(2)}, u32[]{:S(2)}) %collective-permute-start.1) | collective-permute-done | bytes 524320 | tf_op jit(solution)/shard_map/while/body/eval_jaxpr/ppermute | solution.py:10
  410.0 10.0 %collective-permute-done.1 = bf16[4,2,128,256]{3,2,1,0:T(8,128)(2,1)S(1)} collective-permute-done((bf16[4,2,128,256]{3,2,1,0:T(8,128)(2,1)}, bf16[4,2,128,256]{3,2,1,0:T(8,128)(2,1)S(1)}, u32[]{:S(2)}, u32[]{:S(2)}) %collective-permute-start.1) | collective-permute-done | bytes 524320 | tf_op jit(solution)/shard_map/while/body/eval_jaxpr/ppermute | solution.py:10
  422.7 10.0 %collective-permute-done.1 = bf16[4,2,128,256]{3,2,1,0:T(8,128)(2,1)S(1)} collective-permute-done((bf16[4,2,128,256]{3,2,1,0:T(8,128)(2,1)}, bf16[4,2,128,256]{3,2,1,0:T(8,128)(2,1)S(1)}, u32[]{:S(2)}, u32[]{:S(2)}) %collective-permute-start.1) | collective-permute-done | bytes 524320 | tf_op jit(solution)/shard_map/while/body/eval_jaxpr/ppermute | solution.py:10
  435.5 10.0 %collective-permute-done.1 = bf16[4,2,128,256]{3,2,1,0:T(8,128)(2,1)S(1)} collective-permute-done((bf16[4,2,128,256]{3,2,1,0:T(8,128)(2,1)}, bf16[4,2,128,256]{3,2,1,0:T(8,128)(2,1)S(1)}, u32[]{:S(2)}, u32[]{:S(2)}) %collective-permute-start.1) | collective-permute-done | bytes 524320 | tf_op jit(solution)/shard_map/while/body/eval_jaxpr/ppermute | solution.py:10
  448.3 10.0 %collective-permute-done.1 = bf16[4,2,128,256]{3,2,1,0:T(8,128)(2,1)S(1)} collective-permute-done((bf16[4,2,128,256]{3,2,1,0:T(8,128)(2,1)}, bf16[4,2,128,256]{3,2,1,0:T(8,128)(2,1)S(1)}, u32[]{:S(2)}, u32[]{:S(2)}) %collective-permute-start.1) | collective-permute-done | bytes 524320 | tf_op jit(solution)/shard_map/while/body/eval_jaxpr/ppermute | solution.py:10
  461.0 10.0 %collective-permute-done.1 = bf16[4,2,128,256]{3,2,1,0:T(8,128)(2,1)S(1)} collective-permute-done((bf16[4,2,128,256]{3,2,1,0:T(8,128)(2,1)}, bf16[4,2,128,256]{3,2,1,0:T(8,128)(2,1)S(1)}, u32[]{:S(2)}, u32[]{:S(2)}) %collective-permute-start.1) | collective-permute-done | bytes 524320 | tf_op jit(solution)/shard_map/while/body/eval_jaxpr/ppermute | solution.py:10
  473.8 10.0 %collective-permute-done.1 = bf16[4,2,128,256]{3,2,1,0:T(8,128)(2,1)S(1)} collective-permute-done((bf16[4,2,128,256]{3,2,1,0:T(8,128)(2,1)}, bf16[4,2,128,256]{3,2,1,0:T(8,128)(2,1)S(1)}, u32[]{:S(2)}, u32[]{:S(2)}) %collective-permute-start.1) | collective-permute-done | bytes 524320 | tf_op jit(solution)/shard_map/while/body/eval_jaxpr/ppermute | solution.py:10
  486.5 10.0 %collective-permute-done.1 = bf16[4,2,128,256]{3,2,1,0:T(8,128)(2,1)S(1)} collective-permute-done((bf16[4,2,128,256]{3,2,1,0:T(8,128)(2,1)}, bf16[4,2,128,256]{3,2,1,0:T(8,128)(2,1)S(1)}, u32[]{:S(2)}, u32[]{:S(2)}) %collective-permute-start.1) | collective-permute-done | bytes 524320 | tf_op jit(solution)/shard_map/while/body/eval_jaxpr/ppermute | solution.py:10
  (106 shorter events, 90.1 us)
Async XLA Ops:
  7.2 15.2 %copy-start = (bf16[1,4,2,256,256]{4,3,2,1,0:T(8,128)(2,1)S(1)}, bf16[1,4,2,256,256]{4,3,2,1,0:T(8,128)(2,1)}, u32[]{:S(2)}) copy-start(bf16[1,4,2,256,256]{4,3,2,1,0:T(8,128)(2,1)} %param.19) | copy-start | bytes 3145732
  7.2 16.5 %copy-start.7 = (s32[1,4,2]{1,2,0:T(2,128)S(1)}, s32[1,4,2]{1,2,0:T(2,128)}, u32[]{:S(2)}) copy-start(s32[1,4,2]{1,2,0:T(2,128)} %param.25) | copy-start | bytes 100
  7.2 26.6 %copy-start.2 = (bf16[1,4,2,256,256]{4,3,2,1,0:T(8,128)(2,1)S(1)}, bf16[1,4,2,256,256]{4,3,2,1,0:T(8,128)(2,1)}, u32[]{:S(2)}) copy-start(bf16[1,4,2,256,256]{4,3,2,1,0:T(8,128)(2,1)} %param.20) | copy-start | bytes 3145732
  7.2 62.3 %all-gather.3.cloned.1.call-start = ((), (), s32[]{:S(2)}) async-start(), calls=%async_computation | async-start | bytes 4718592 | tf_op jit(solution)/shard_map/all_gather | solution.py:114
  7.9 68.0 %collective-permute-start.3 = (bf16[1,4,2,128,256]{4,3,2,1,0:T(8,128)(2,1)}, bf16[1,4,2,128,256]{4,3,2,1,0:T(8,128)(2,1)}, u32[]{:S(2)}, u32[]{:S(2)}) collective-permute-start(bf16[1,4,2,128,256]{4,3,2,1,0:T(8,128)(2,1)} %param.18), channel_id=1, source_target_pairs={{16,0},{32,16},{48,32},{64,48},{80,64},{96,80},{112,96},{128,112},... | collective-permute-start | bytes 1572872 | tf_op jit(solution)/shard_map/ppermute | solution.py:21
  10.5 23.3 %collective-permute-start.2 = (bf16[1,4,2,128,256]{4,3,2,1,0:T(8,128)(2,1)}, bf16[1,4,2,128,256]{4,3,2,1,0:T(8,128)(2,1)}, u32[]{:S(2)}, u32[]{:S(2)}) collective-permute-start(bf16[1,4,2,128,256]{4,3,2,1,0:T(8,128)(2,1)} %param.18), channel_id=1, source_target_pairs={{0,16},{16,32},{32,48},{48,64},{64,80},{80,96},{96,112},{112,128},... | collective-permute-start | bytes 1572872 | tf_op jit(solution)/shard_map/ppermute | solution.py:18
  17.0 14.2 %collective-permute-start.4 = (bf16[4,1,128,256]{3,2,1,0:T(8,128)(2,1)}, bf16[4,1,128,256]{3,2,1,0:T(8,128)(2,1)}, u32[]{:S(2)}, u32[]{:S(2)}) collective-permute-start(bf16[4,1,128,256]{3,2,1,0:T(8,128)(2,1)} %get-tuple-element.314), channel_id=1, source_target_pairs={{0,1},{2,3},{4,5},{6,7},{8,9},{10,11},{12,13},{14,15},{16,17},{18,... | collective-permute-start | bytes 786440 | tf_op jit(solution)/shard_map/ppermute | solution.py:10
  69.5 6.4 %copy-start.3 = (bf16[1,4,2,256,256]{4,3,2,1,0:T(8,128)(2,1)S(1)}, bf16[1,4,2,256,256]{4,3,2,1,0:T(8,128)(2,1)}, u32[]{:S(2)}) copy-start(bf16[1,4,2,256,256]{4,3,2,1,0:T(8,128)(2,1)} %param.21) | copy-start | bytes 3145732
  69.6 6.4 %copy-start.4 = (f32[4,2,128,256]{3,2,1,0:T(8,128)S(1)}, f32[4,2,128,256]{3,2,1,0:T(8,128)}, u32[]{:S(2)}) copy-start(f32[4,2,128,256]{3,2,1,0:T(8,128)} %convolution_add_fusion.1) | copy-start | bytes 3145732
  69.6 6.4 %copy-start.5 = (f32[4,2,128,256]{3,2,1,0:T(8,128)S(1)}, f32[4,2,128,256]{3,2,1,0:T(8,128)}, u32[]{:S(2)}) copy-start(f32[4,2,128,256]{3,2,1,0:T(8,128)} %fusion.10) | copy-start | bytes 3145732
  74.3 5.8 %copy-start.1 = (bf16[1,4,2,256,256]{4,3,2,1,0:T(8,128)(2,1)S(1)}, bf16[1,4,2,256,256]{4,3,2,1,0:T(8,128)(2,1)}, u32[]{:S(2)}) copy-start(bf16[1,4,2,256,256]{4,3,2,1,0:T(8,128)(2,1)} %param.22) | copy-start | bytes 3145732
  81.0 11.5 %collective-permute-start = (bf16[4,2,128,256]{3,2,1,0:T(8,128)(2,1)}, bf16[4,2,128,256]{3,2,1,0:T(8,128)(2,1)}, u32[]{:S(2)}, u32[]{:S(2)}) collective-permute-start(bf16[4,2,128,256]{3,2,1,0:T(8,128)(2,1)} %get-tuple-element.399), channel_id=1, source_target_pairs={{0,16},{16,32},{32,48},{48,64},{64,80},{80,96},{96,112},{112,128},... | collective-permute-start | bytes 1572872 | tf_op jit(solution)/shard_map/while/body/eval_jaxpr/ppermute | solution.py:10
  93.3 12.0 %collective-permute-start = (bf16[4,2,128,256]{3,2,1,0:T(8,128)(2,1)}, bf16[4,2,128,256]{3,2,1,0:T(8,128)(2,1)}, u32[]{:S(2)}, u32[]{:S(2)}) collective-permute-start(bf16[4,2,128,256]{3,2,1,0:T(8,128)(2,1)} %get-tuple-element.399), channel_id=1, source_target_pairs={{0,16},{16,32},{32,48},{48,64},{64,80},{80,96},{96,112},{112,128},... | collective-permute-start | bytes 1572872 | tf_op jit(solution)/shard_map/while/body/eval_jaxpr/ppermute | solution.py:10
  106.2 12.0 %collective-permute-start = (bf16[4,2,128,256]{3,2,1,0:T(8,128)(2,1)}, bf16[4,2,128,256]{3,2,1,0:T(8,128)(2,1)}, u32[]{:S(2)}, u32[]{:S(2)}) collective-permute-start(bf16[4,2,128,256]{3,2,1,0:T(8,128)(2,1)} %get-tuple-element.399), channel_id=1, source_target_pairs={{0,16},{16,32},{32,48},{48,64},{64,80},{80,96},{96,112},{112,128},... | collective-permute-start | bytes 1572872 | tf_op jit(solution)/shard_map/while/body/eval_jaxpr/ppermute | solution.py:10
  119.0 12.0 %collective-permute-start = (bf16[4,2,128,256]{3,2,1,0:T(8,128)(2,1)}, bf16[4,2,128,256]{3,2,1,0:T(8,128)(2,1)}, u32[]{:S(2)}, u32[]{:S(2)}) collective-permute-start(bf16[4,2,128,256]{3,2,1,0:T(8,128)(2,1)} %get-tuple-element.399), channel_id=1, source_target_pairs={{0,16},{16,32},{32,48},{48,64},{64,80},{80,96},{96,112},{112,128},... | collective-permute-start | bytes 1572872 | tf_op jit(solution)/shard_map/while/body/eval_jaxpr/ppermute | solution.py:10
  131.9 12.0 %collective-permute-start = (bf16[4,2,128,256]{3,2,1,0:T(8,128)(2,1)}, bf16[4,2,128,256]{3,2,1,0:T(8,128)(2,1)}, u32[]{:S(2)}, u32[]{:S(2)}) collective-permute-start(bf16[4,2,128,256]{3,2,1,0:T(8,128)(2,1)} %get-tuple-element.399), channel_id=1, source_target_pairs={{0,16},{16,32},{32,48},{48,64},{64,80},{80,96},{96,112},{112,128},... | collective-permute-start | bytes 1572872 | tf_op jit(solution)/shard_map/while/body/eval_jaxpr/ppermute | solution.py:10
  144.7 12.0 %collective-permute-start = (bf16[4,2,128,256]{3,2,1,0:T(8,128)(2,1)}, bf16[4,2,128,256]{3,2,1,0:T(8,128)(2,1)}, u32[]{:S(2)}, u32[]{:S(2)}) collective-permute-start(bf16[4,2,128,256]{3,2,1,0:T(8,128)(2,1)} %get-tuple-element.399), channel_id=1, source_target_pairs={{0,16},{16,32},{32,48},{48,64},{64,80},{80,96},{96,112},{112,128},... | collective-permute-start | bytes 1572872 | tf_op jit(solution)/shard_map/while/body/eval_jaxpr/ppermute | solution.py:10
  157.6 12.0 %collective-permute-start = (bf16[4,2,128,256]{3,2,1,0:T(8,128)(2,1)}, bf16[4,2,128,256]{3,2,1,0:T(8,128)(2,1)}, u32[]{:S(2)}, u32[]{:S(2)}) collective-permute-start(bf16[4,2,128,256]{3,2,1,0:T(8,128)(2,1)} %get-tuple-element.399), channel_id=1, source_target_pairs={{0,16},{16,32},{32,48},{48,64},{64,80},{80,96},{96,112},{112,128},... | collective-permute-start | bytes 1572872 | tf_op jit(solution)/shard_map/while/body/eval_jaxpr/ppermute | solution.py:10
  173.9 8.5 %collective-permute-start = (bf16[4,2,128,256]{3,2,1,0:T(8,128)(2,1)}, bf16[4,2,128,256]{3,2,1,0:T(8,128)(2,1)}, u32[]{:S(2)}, u32[]{:S(2)}) collective-permute-start(bf16[4,2,128,256]{3,2,1,0:T(8,128)(2,1)} %get-tuple-element.399), channel_id=1, source_target_pairs={{0,16},{16,32},{32,48},{48,64},{64,80},{80,96},{96,112},{112,128},... | collective-permute-start | bytes 1572872 | tf_op jit(solution)/shard_map/while/body/eval_jaxpr/ppermute | solution.py:10
  183.3 15.5 %collective-permute-start = (bf16[4,2,128,256]{3,2,1,0:T(8,128)(2,1)}, bf16[4,2,128,256]{3,2,1,0:T(8,128)(2,1)}, u32[]{:S(2)}, u32[]{:S(2)}) collective-permute-start(bf16[4,2,128,256]{3,2,1,0:T(8,128)(2,1)} %get-tuple-element.399), channel_id=1, source_target_pairs={{0,16},{16,32},{32,48},{48,64},{64,80},{80,96},{96,112},{112,128},... | collective-permute-start | bytes 1572872 | tf_op jit(solution)/shard_map/while/body/eval_jaxpr/ppermute | solution.py:10
  199.6 12.0 %collective-permute-start = (bf16[4,2,128,256]{3,2,1,0:T(8,128)(2,1)}, bf16[4,2,128,256]{3,2,1,0:T(8,128)(2,1)}, u32[]{:S(2)}, u32[]{:S(2)}) collective-permute-start(bf16[4,2,128,256]{3,2,1,0:T(8,128)(2,1)} %get-tuple-element.399), channel_id=1, source_target_pairs={{0,16},{16,32},{32,48},{48,64},{64,80},{80,96},{96,112},{112,128},... | collective-permute-start | bytes 1572872 | tf_op jit(solution)/shard_map/while/body/eval_jaxpr/ppermute | solution.py:10
  212.5 12.0 %collective-permute-start = (bf16[4,2,128,256]{3,2,1,0:T(8,128)(2,1)}, bf16[4,2,128,256]{3,2,1,0:T(8,128)(2,1)}, u32[]{:S(2)}, u32[]{:S(2)}) collective-permute-start(bf16[4,2,128,256]{3,2,1,0:T(8,128)(2,1)} %get-tuple-element.399), channel_id=1, source_target_pairs={{0,16},{16,32},{32,48},{48,64},{64,80},{80,96},{96,112},{112,128},... | collective-permute-start | bytes 1572872 | tf_op jit(solution)/shard_map/while/body/eval_jaxpr/ppermute | solution.py:10
  225.3 12.0 %collective-permute-start = (bf16[4,2,128,256]{3,2,1,0:T(8,128)(2,1)}, bf16[4,2,128,256]{3,2,1,0:T(8,128)(2,1)}, u32[]{:S(2)}, u32[]{:S(2)}) collective-permute-start(bf16[4,2,128,256]{3,2,1,0:T(8,128)(2,1)} %get-tuple-element.399), channel_id=1, source_target_pairs={{0,16},{16,32},{32,48},{48,64},{64,80},{80,96},{96,112},{112,128},... | collective-permute-start | bytes 1572872 | tf_op jit(solution)/shard_map/while/body/eval_jaxpr/ppermute | solution.py:10
  238.2 12.0 %collective-permute-start = (bf16[4,2,128,256]{3,2,1,0:T(8,128)(2,1)}, bf16[4,2,128,256]{3,2,1,0:T(8,128)(2,1)}, u32[]{:S(2)}, u32[]{:S(2)}) collective-permute-start(bf16[4,2,128,256]{3,2,1,0:T(8,128)(2,1)} %get-tuple-element.399), channel_id=1, source_target_pairs={{0,16},{16,32},{32,48},{48,64},{64,80},{80,96},{96,112},{112,128},... | collective-permute-start | bytes 1572872 | tf_op jit(solution)/shard_map/while/body/eval_jaxpr/ppermute | solution.py:10
  251.0 12.0 %collective-permute-start = (bf16[4,2,128,256]{3,2,1,0:T(8,128)(2,1)}, bf16[4,2,128,256]{3,2,1,0:T(8,128)(2,1)}, u32[]{:S(2)}, u32[]{:S(2)}) collective-permute-start(bf16[4,2,128,256]{3,2,1,0:T(8,128)(2,1)} %get-tuple-element.399), channel_id=1, source_target_pairs={{0,16},{16,32},{32,48},{48,64},{64,80},{80,96},{96,112},{112,128},... | collective-permute-start | bytes 1572872 | tf_op jit(solution)/shard_map/while/body/eval_jaxpr/ppermute | solution.py:10
  263.9 12.0 %collective-permute-start = (bf16[4,2,128,256]{3,2,1,0:T(8,128)(2,1)}, bf16[4,2,128,256]{3,2,1,0:T(8,128)(2,1)}, u32[]{:S(2)}, u32[]{:S(2)}) collective-permute-start(bf16[4,2,128,256]{3,2,1,0:T(8,128)(2,1)} %get-tuple-element.399), channel_id=1, source_target_pairs={{0,16},{16,32},{32,48},{48,64},{64,80},{80,96},{96,112},{112,128},... | collective-permute-start | bytes 1572872 | tf_op jit(solution)/shard_map/while/body/eval_jaxpr/ppermute | solution.py:10
  276.7 12.0 %collective-permute-start = (bf16[4,2,128,256]{3,2,1,0:T(8,128)(2,1)}, bf16[4,2,128,256]{3,2,1,0:T(8,128)(2,1)}, u32[]{:S(2)}, u32[]{:S(2)}) collective-permute-start(bf16[4,2,128,256]{3,2,1,0:T(8,128)(2,1)} %get-tuple-element.399), channel_id=1, source_target_pairs={{0,16},{16,32},{32,48},{48,64},{64,80},{80,96},{96,112},{112,128},... | collective-permute-start | bytes 1572872 | tf_op jit(solution)/shard_map/while/body/eval_jaxpr/ppermute | solution.py:10
  289.7 12.7 %collective-permute-start.1 = (bf16[4,2,128,256]{3,2,1,0:T(8,128)(2,1)}, bf16[4,2,128,256]{3,2,1,0:T(8,128)(2,1)S(1)}, u32[]{:S(2)}, u32[]{:S(2)}) collective-permute-start(bf16[4,2,128,256]{3,2,1,0:T(8,128)(2,1)} %get-tuple-element.408), channel_id=1, source_target_pairs={{16,0},{32,16},{48,32},{64,48},{80,64},{96,80},{112,96},{128,112},... | collective-permute-start | bytes 1572872 | tf_op jit(solution)/shard_map/while/body/eval_jaxpr/ppermute | solution.py:10
  303.2 11.9 %collective-permute-start.1 = (bf16[4,2,128,256]{3,2,1,0:T(8,128)(2,1)}, bf16[4,2,128,256]{3,2,1,0:T(8,128)(2,1)S(1)}, u32[]{:S(2)}, u32[]{:S(2)}) collective-permute-start(bf16[4,2,128,256]{3,2,1,0:T(8,128)(2,1)} %get-tuple-element.408), channel_id=1, source_target_pairs={{16,0},{32,16},{48,32},{64,48},{80,64},{96,80},{112,96},{128,112},... | collective-permute-start | bytes 1572872 | tf_op jit(solution)/shard_map/while/body/eval_jaxpr/ppermute | solution.py:10
  316.0 11.9 %collective-permute-start.1 = (bf16[4,2,128,256]{3,2,1,0:T(8,128)(2,1)}, bf16[4,2,128,256]{3,2,1,0:T(8,128)(2,1)S(1)}, u32[]{:S(2)}, u32[]{:S(2)}) collective-permute-start(bf16[4,2,128,256]{3,2,1,0:T(8,128)(2,1)} %get-tuple-element.408), channel_id=1, source_target_pairs={{16,0},{32,16},{48,32},{64,48},{80,64},{96,80},{112,96},{128,112},... | collective-permute-start | bytes 1572872 | tf_op jit(solution)/shard_map/while/body/eval_jaxpr/ppermute | solution.py:10
  328.7 11.9 %collective-permute-start.1 = (bf16[4,2,128,256]{3,2,1,0:T(8,128)(2,1)}, bf16[4,2,128,256]{3,2,1,0:T(8,128)(2,1)S(1)}, u32[]{:S(2)}, u32[]{:S(2)}) collective-permute-start(bf16[4,2,128,256]{3,2,1,0:T(8,128)(2,1)} %get-tuple-element.408), channel_id=1, source_target_pairs={{16,0},{32,16},{48,32},{64,48},{80,64},{96,80},{112,96},{128,112},... | collective-permute-start | bytes 1572872 | tf_op jit(solution)/shard_map/while/body/eval_jaxpr/ppermute | solution.py:10
  341.5 11.9 %collective-permute-start.1 = (bf16[4,2,128,256]{3,2,1,0:T(8,128)(2,1)}, bf16[4,2,128,256]{3,2,1,0:T(8,128)(2,1)S(1)}, u32[]{:S(2)}, u32[]{:S(2)}) collective-permute-start(bf16[4,2,128,256]{3,2,1,0:T(8,128)(2,1)} %get-tuple-element.408), channel_id=1, source_target_pairs={{16,0},{32,16},{48,32},{64,48},{80,64},{96,80},{112,96},{128,112},... | collective-permute-start | bytes 1572872 | tf_op jit(solution)/shard_map/while/body/eval_jaxpr/ppermute | solution.py:10
  354.2 11.9 %collective-permute-start.1 = (bf16[4,2,128,256]{3,2,1,0:T(8,128)(2,1)}, bf16[4,2,128,256]{3,2,1,0:T(8,128)(2,1)S(1)}, u32[]{:S(2)}, u32[]{:S(2)}) collective-permute-start(bf16[4,2,128,256]{3,2,1,0:T(8,128)(2,1)} %get-tuple-element.408), channel_id=1, source_target_pairs={{16,0},{32,16},{48,32},{64,48},{80,64},{96,80},{112,96},{128,112},... | collective-permute-start | bytes 1572872 | tf_op jit(solution)/shard_map/while/body/eval_jaxpr/ppermute | solution.py:10
  367.0 11.9 %collective-permute-start.1 = (bf16[4,2,128,256]{3,2,1,0:T(8,128)(2,1)}, bf16[4,2,128,256]{3,2,1,0:T(8,128)(2,1)S(1)}, u32[]{:S(2)}, u32[]{:S(2)}) collective-permute-start(bf16[4,2,128,256]{3,2,1,0:T(8,128)(2,1)} %get-tuple-element.408), channel_id=1, source_target_pairs={{16,0},{32,16},{48,32},{64,48},{80,64},{96,80},{112,96},{128,112},... | collective-permute-start | bytes 1572872 | tf_op jit(solution)/shard_map/while/body/eval_jaxpr/ppermute | solution.py:10
  379.7 11.9 %collective-permute-start.1 = (bf16[4,2,128,256]{3,2,1,0:T(8,128)(2,1)}, bf16[4,2,128,256]{3,2,1,0:T(8,128)(2,1)S(1)}, u32[]{:S(2)}, u32[]{:S(2)}) collective-permute-start(bf16[4,2,128,256]{3,2,1,0:T(8,128)(2,1)} %get-tuple-element.408), channel_id=1, source_target_pairs={{16,0},{32,16},{48,32},{64,48},{80,64},{96,80},{112,96},{128,112},... | collective-permute-start | bytes 1572872 | tf_op jit(solution)/shard_map/while/body/eval_jaxpr/ppermute | solution.py:10
  395.3 11.9 %collective-permute-start.1 = (bf16[4,2,128,256]{3,2,1,0:T(8,128)(2,1)}, bf16[4,2,128,256]{3,2,1,0:T(8,128)(2,1)S(1)}, u32[]{:S(2)}, u32[]{:S(2)}) collective-permute-start(bf16[4,2,128,256]{3,2,1,0:T(8,128)(2,1)} %get-tuple-element.408), channel_id=1, source_target_pairs={{16,0},{32,16},{48,32},{64,48},{80,64},{96,80},{112,96},{128,112},... | collective-permute-start | bytes 1572872 | tf_op jit(solution)/shard_map/while/body/eval_jaxpr/ppermute | solution.py:10
  408.1 11.9 %collective-permute-start.1 = (bf16[4,2,128,256]{3,2,1,0:T(8,128)(2,1)}, bf16[4,2,128,256]{3,2,1,0:T(8,128)(2,1)S(1)}, u32[]{:S(2)}, u32[]{:S(2)}) collective-permute-start(bf16[4,2,128,256]{3,2,1,0:T(8,128)(2,1)} %get-tuple-element.408), channel_id=1, source_target_pairs={{16,0},{32,16},{48,32},{64,48},{80,64},{96,80},{112,96},{128,112},... | collective-permute-start | bytes 1572872 | tf_op jit(solution)/shard_map/while/body/eval_jaxpr/ppermute | solution.py:10
  420.8 11.9 %collective-permute-start.1 = (bf16[4,2,128,256]{3,2,1,0:T(8,128)(2,1)}, bf16[4,2,128,256]{3,2,1,0:T(8,128)(2,1)S(1)}, u32[]{:S(2)}, u32[]{:S(2)}) collective-permute-start(bf16[4,2,128,256]{3,2,1,0:T(8,128)(2,1)} %get-tuple-element.408), channel_id=1, source_target_pairs={{16,0},{32,16},{48,32},{64,48},{80,64},{96,80},{112,96},{128,112},... | collective-permute-start | bytes 1572872 | tf_op jit(solution)/shard_map/while/body/eval_jaxpr/ppermute | solution.py:10
  433.6 11.9 %collective-permute-start.1 = (bf16[4,2,128,256]{3,2,1,0:T(8,128)(2,1)}, bf16[4,2,128,256]{3,2,1,0:T(8,128)(2,1)S(1)}, u32[]{:S(2)}, u32[]{:S(2)}) collective-permute-start(bf16[4,2,128,256]{3,2,1,0:T(8,128)(2,1)} %get-tuple-element.408), channel_id=1, source_target_pairs={{16,0},{32,16},{48,32},{64,48},{80,64},{96,80},{112,96},{128,112},... | collective-permute-start | bytes 1572872 | tf_op jit(solution)/shard_map/while/body/eval_jaxpr/ppermute | solution.py:10
  446.3 11.9 %collective-permute-start.1 = (bf16[4,2,128,256]{3,2,1,0:T(8,128)(2,1)}, bf16[4,2,128,256]{3,2,1,0:T(8,128)(2,1)S(1)}, u32[]{:S(2)}, u32[]{:S(2)}) collective-permute-start(bf16[4,2,128,256]{3,2,1,0:T(8,128)(2,1)} %get-tuple-element.408), channel_id=1, source_target_pairs={{16,0},{32,16},{48,32},{64,48},{80,64},{96,80},{112,96},{128,112},... | collective-permute-start | bytes 1572872 | tf_op jit(solution)/shard_map/while/body/eval_jaxpr/ppermute | solution.py:10
  459.1 11.9 %collective-permute-start.1 = (bf16[4,2,128,256]{3,2,1,0:T(8,128)(2,1)}, bf16[4,2,128,256]{3,2,1,0:T(8,128)(2,1)S(1)}, u32[]{:S(2)}, u32[]{:S(2)}) collective-permute-start(bf16[4,2,128,256]{3,2,1,0:T(8,128)(2,1)} %get-tuple-element.408), channel_id=1, source_target_pairs={{16,0},{32,16},{48,32},{64,48},{80,64},{96,80},{112,96},{128,112},... | collective-permute-start | bytes 1572872 | tf_op jit(solution)/shard_map/while/body/eval_jaxpr/ppermute | solution.py:10
  471.8 11.9 %collective-permute-start.1 = (bf16[4,2,128,256]{3,2,1,0:T(8,128)(2,1)}, bf16[4,2,128,256]{3,2,1,0:T(8,128)(2,1)S(1)}, u32[]{:S(2)}, u32[]{:S(2)}) collective-permute-start(bf16[4,2,128,256]{3,2,1,0:T(8,128)(2,1)} %get-tuple-element.408), channel_id=1, source_target_pairs={{16,0},{32,16},{48,32},{64,48},{80,64},{96,80},{112,96},{128,112},... | collective-permute-start | bytes 1572872 | tf_op jit(solution)/shard_map/while/body/eval_jaxpr/ppermute | solution.py:10
  484.6 11.9 %collective-permute-start.1 = (bf16[4,2,128,256]{3,2,1,0:T(8,128)(2,1)}, bf16[4,2,128,256]{3,2,1,0:T(8,128)(2,1)S(1)}, u32[]{:S(2)}, u32[]{:S(2)}) collective-permute-start(bf16[4,2,128,256]{3,2,1,0:T(8,128)(2,1)} %get-tuple-element.408), channel_id=1, source_target_pairs={{16,0},{32,16},{48,32},{64,48},{80,64},{96,80},{112,96},{128,112},... | collective-permute-start | bytes 1572872 | tf_op jit(solution)/shard_map/while/body/eval_jaxpr/ppermute | solution.py:10
  496.5 0.8 copy-start.6
Sparse Core Ops, SparseCore 0:
  9.8 59.6 all-gather.2
where the time goes:
time: 506 us; the launch traced here: 504 us
  waiting for transfers between devices  305 us (60%)
  starting transfers between devices  132 us (26%)
  local copies, waits for them, and re-layouts  32.5 us (6%)
  matrix products  20.2 us (4%)
  between operations  14.1 us (3%)
    ppermute x33, waiting for transfers between devices, from_behind(): return lax.ppermute(value, axis, pairs)  271 us
    ppermute x33, starting transfers between devices, from_behind(): return lax.ppermute(value, axis, pairs)  125 us
    all_gather x1, waiting for transfers between devices, local(): piece = lax.all_gather(current, 'valley', axis=0, tiled=True)  33.4 us
    another operation x34, local copies, waits for them, and re-layouts  26.9 us
    dot_general x7, matrix products, apply_blocks(): jnp.einsum('bqrs,bqst->bqrt', vectors, blocks, preferred_element_type=jnp...  15.5 us
  transfers between devices with their start and end apart: 36, of which 34 were waited for; matrix products, arithmetic and copies ran while one was open for 3% of the time, Pallas kernels for 0%

commit v1 on v0

v1 whole, which is shorter than its diff:
```python
import functools

import jax
import jax.numpy as jnp
from jax import lax
from jax.experimental import pallas as pl
from jax.experimental.pallas import tpu as pltpu
from jax.sharding import PartitionSpec as P

MESH = pl.DeviceIdType.MESH
ROW_SPLIT = 2


def with_halo(block, sides, width):
    for axis, dim in sides:
        count = lax.axis_size(axis)
        forward = [(i, i + 1) for i in range(count - 1)]
        backward = [(target, source) for source, target in forward]
        low = lax.ppermute(
            lax.slice_in_dim(block, block.shape[dim] - width, None, axis=dim), axis, forward
        )
        high = lax.ppermute(lax.slice_in_dim(block, 0, width, axis=dim), axis, backward)
        block = jnp.concatenate([low, block, high], axis=dim)
    return block


def from_behind(value, axis, by):
    length = lax.axis_size(axis)
    pairs = [(i, i + by) for i in range(length) if 0 <= i + by < length]
    return lax.ppermute(value, axis, pairs)


def apply_blocks(vectors, blocks):
    return jnp.einsum("bqrs,bqst->bqrt", vectors, blocks, preferred_element_type=jnp.float32)


def sweep_kernel(
    resid_ref,
    lower_ref,
    upper_ref,
    pivot_ref,
    out_ref,
    fronts,
    fwd_buf,
    bwd_buf,
    fsend,
    frecv,
    bsend,
    brecv,
    *,
    n,
    per_block,
):
    f32 = jnp.float32
    bf16 = jnp.bfloat16
    h = lax.axis_index("elev")
    v = lax.axis_index("valley")
    d = lax.axis_index("down")
    chunks = resid_ref.shape[0]
    has_below = h > 0
    has_above = h < n - 1

    barrier = pltpu.get_barrier_semaphore()

    @pl.when(has_below)
    def _():
        pl.semaphore_signal(barrier, 1, device_id=(h - 1, v, d), device_id_type=MESH)

    @pl.when(has_above)
    def _():
        pl.semaphore_signal(barrier, 1, device_id=(h + 1, v, d), device_id_type=MESH)

    pl.semaphore_wait(barrier, has_below.astype(jnp.int32) + has_above.astype(jnp.int32))

    def fwd_copy(g):
        return pltpu.make_async_remote_copy(
            src_ref=fronts.at[g],
            dst_ref=fwd_buf.at[g],
            send_sem=fsend.at[g],
            recv_sem=frecv.at[g],
            device_id=(h + 1, v, d),
            device_id_type=MESH,
        )

    def bwd_copy(g):
        return pltpu.make_async_remote_copy(
            src_ref=out_ref.at[g],
            dst_ref=bwd_buf.at[g],
            send_sem=bsend.at[g],
            recv_sem=brecv.at[g],
            device_id=(h - 1, v, d),
            device_id_type=MESH,
        )

    def fwd_body(g, carry):
        blk = g // per_block

        @pl.when(has_below)
        def _():
            fwd_copy(g).wait_recv()
            inner = resid_ref[g].astype(f32) - jnp.dot(
                fwd_buf[g], lower_ref[blk], preferred_element_type=f32
            )
            fronts[g] = jnp.dot(
                inner.astype(bf16), pivot_ref[blk], preferred_element_type=f32
            ).astype(bf16)

        @pl.when(jnp.logical_not(has_below))
        def _():
            fronts[g] = jnp.dot(resid_ref[g], pivot_ref[blk], preferred_element_type=f32).astype(
                bf16
            )

        @pl.when(has_above)
        def _():
            fwd_copy(g).start()

        return carry

    lax.fori_loop(0, chunks, fwd_body, 0)

    def bwd_body(g, carry):
        blk = g // per_block

        @pl.when(has_above)
        def _():
            bwd_copy(g).wait_recv()
            carried = jnp.dot(bwd_buf[g], upper_ref[blk], preferred_element_type=f32).astype(bf16)
            out_ref[g] = (
                fronts[g].astype(f32) - jnp.dot(carried, pivot_ref[blk], preferred_element_type=f32)
            ).astype(bf16)

        @pl.when(jnp.logical_not(has_above))
        def _():
            out_ref[g] = fronts[g]

        @pl.when(has_below)
        def _():
            bwd_copy(g).start()

        return carry

    lax.fori_loop(0, chunks, bwd_body, 0)

    def drain(g, carry):
        @pl.when(has_above)
        def _():
            fwd_copy(g).wait_send()

        @pl.when(has_below)
        def _():
            bwd_copy(g).wait_send()

        return carry

    lax.fori_loop(0, chunks, drain, 0)


def sweep(resid_l, lower_l, upper_l, pivot_l):
    n = lax.axis_size("elev")
    chunks, rows, width = resid_l.shape
    per_block = chunks // lower_l.shape[0]
    vmem = pl.BlockSpec(memory_space=pltpu.VMEM)
    flops = 4 * chunks * rows * width * width
    weight_bytes = 3 * lower_l.size * lower_l.dtype.itemsize
    return pl.pallas_call(
        functools.partial(sweep_kernel, n=n, per_block=per_block),
        out_shape=jax.ShapeDtypeStruct(resid_l.shape, resid_l.dtype),
        in_specs=[vmem] * 4,
        out_specs=vmem,
        scratch_shapes=[
            pltpu.VMEM(resid_l.shape, resid_l.dtype),
            pltpu.VMEM(resid_l.shape, resid_l.dtype),
            pltpu.VMEM(resid_l.shape, resid_l.dtype),
            pltpu.SemaphoreType.DMA((chunks,)),
            pltpu.SemaphoreType.DMA((chunks,)),
            pltpu.SemaphoreType.DMA((chunks,)),
            pltpu.SemaphoreType.DMA((chunks,)),
        ],
        compiler_params=pltpu.CompilerParams(collective_id=0, has_side_effects=True),
        cost_estimate=pl.CostEstimate(
            flops=flops, bytes_accessed=weight_bytes + 2 * resid_l.size * 2, transcendentals=0
        ),
    )(resid_l, lower_l, upper_l, pivot_l)


def local(
    resid,
    direction,
    diag_blocks,
    lower_blocks,
    upper_blocks,
    inv_pivots,
    down_coupling,
    valley_coupling,
    coupled_column,
):
    lower_local = lower_blocks[0]
    upper_local = upper_blocks[0]
    pivot_local = inv_pivots[0]
    va, dc, nr, bs = resid.shape[1:]
    blocks = va * dc
    chunk_shape = (blocks * ROW_SPLIT, nr // ROW_SPLIT, bs)
    solved = sweep(
        resid[0].reshape(chunk_shape),
        lower_local.reshape(blocks, bs, bs),
        upper_local.reshape(blocks, bs, bs),
        pivot_local.reshape(blocks, bs, bs),
    ).reshape(resid.shape)

    current = direction[0]
    padded = with_halo(direction, (("elev", 0),), 1)
    below_dir = padded[0]
    above_dir = padded[2]
    rim_blocks = from_behind(current[:, -1:], "down", 1)
    upstream = jnp.concatenate([rim_blocks, current[:, :-1]], axis=1)
    partner_index = coupled_column[0]
    piece = lax.all_gather(current, "valley", axis=0, tiled=True)
    count = piece.shape[0]
    columns = jnp.arange(count, dtype=jnp.int32)
    picker = (partner_index[:, :, None] == columns[None, None, :]).astype(jnp.bfloat16)
    partner_sum = jnp.einsum("pqc,cqrs->pqrs", picker, piece, preferred_element_type=jnp.float32)
    partner = partner_sum.astype(jnp.bfloat16)
    total = apply_blocks(current, diag_blocks[0])
    total = total + apply_blocks(below_dir, lower_local)
    total = total + apply_blocks(above_dir, upper_local)
    total = total + apply_blocks(upstream, down_coupling[0])
    total = total + apply_blocks(partner, valley_coupling[0])
    return (solved, total[None])


def solution(mesh):
    spec = P("elev", "valley", "down", None, None)
    in_specs = (spec,) * 8 + (P("elev", "valley", "down"),)
    out_specs = (spec, spec)
    return jax.shard_map(local, mesh=mesh, in_specs=in_specs, out_specs=out_specs, check_vma=False)
```

time: 506 us -> 119 us (0.24)
  the two profiles are of different devices: /device:TPU:97 before, /device:TPU:1 now
where the time goes in v1:
time: 119 us
  Pallas kernels  74.9 us (63%)
  between operations  14.1 us (12%)
  matrix products  13.8 us (12%)
  starting transfers between devices  12.4 us (10%)
  local copies, waits for them, and re-layouts  2.7 us (2%)
    pallas_call x1, Pallas kernels, sweep(): pl.pallas_call(functools.partial(sweep_kernel, n=n, per_block=per_block),...  74.9 us
    dot_general x5, matrix products, apply_blocks(): jnp.einsum('bqrs,bqst->bqrt', vectors, blocks, preferred_element_type=jnp...  8.96 us
    ppermute x1, starting transfers between devices, from_behind(): return lax.ppermute(value, axis, pairs)  5.28 us
    ppermute x1, starting transfers between devices, with_halo(): lax.ppermute(lax.slice_in_dim(block, 0, width, axis=dim), axis, backward)  5.15 us
    dot_general x1, matrix products, local(): jnp.einsum('pqc,cqrs->pqrs', picker, piece, preferred_element_type=jnp.fl...  4.79 us
  transfers between devices with their start and end apart: 4, of which 0 were waited for; matrix products, arithmetic and copies ran while one was open for 11% of the time, Pallas kernels for 63%

profile of v1, /device:TPU:1, one launch (start us, length us, event | category | flops | bytes accessed | tf_op | source)
XLA Modules:
  0.0 118.7 jit_solution(8676035933270645832)
XLA Ops:
  7.2 0.0 copy-start
  7.2 0.0 copy-start.7
  7.2 0.0 all-gather.3.cloned.1.call-start
  7.2 0.7 all-gather.3.cloned.1.call-update
  7.9 5.2 %collective-permute-start.1 = (bf16[1,4,2,128,256]{4,3,2,1,0:T(8,128)(2,1)}, bf16[1,4,2,128,256]{4,3,2,1,0:T(8,128)(2,1)}, u32[]{:S(2)}, u32[]{:S(2)}) collective-permute-start(bf16[1,4,2,128,256]{4,3,2,1,0:T(8,128)(2,1)} %param.10), channel_id=1, source_target_pairs={{16,0},{32,16},{48,32},{64,48},{80,64},{96,80},{112,96},{128,112},... | collective-permute-start | bytes 1572872 | tf_op jit(solution)/shard_map/ppermute | solution.py:22
  13.1 1.9 %collective-permute-start = (bf16[1,4,2,128,256]{4,3,2,1,0:T(8,128)(2,1)}, bf16[1,4,2,128,256]{4,3,2,1,0:T(8,128)(2,1)}, u32[]{:S(2)}, u32[]{:S(2)}) collective-permute-start(bf16[1,4,2,128,256]{4,3,2,1,0:T(8,128)(2,1)} %param.10), channel_id=1, source_target_pairs={{0,16},{16,32},{32,48},{48,64},{64,80},{80,96},{96,112},{112,128},... | collective-permute-start | bytes 1572872 | tf_op jit(solution)/shard_map/ppermute | solution.py:19
  15.0 1.8 %fusion.23 = (bf16[4,1,128,256]{3,2,1,0:T(8,128)(2,1)}, bf16[4,1,128,256]{3,2,1,0:T(8,128)(2,1)S(1)}) fusion(bf16[4,2,128,256]{3,2,1,0:T(8,128)(2,1)} %bitcast.40), kind=kLoop, calls=%fused_computation.26 | loop fusion | bytes 1048576 | tf_op jit(solution)/shard_map/slice | solution.py:215
  16.8 0.0 copy-start.1
  16.8 5.3 %collective-permute-start.2 = (bf16[4,1,128,256]{3,2,1,0:T(8,128)(2,1)}, bf16[4,1,128,256]{3,2,1,0:T(8,128)(2,1)}, u32[]{:S(2)}, u32[]{:S(2)}) collective-permute-start(bf16[4,1,128,256]{3,2,1,0:T(8,128)(2,1)} %get-tuple-element.2), channel_id=1, source_target_pairs={{0,1},{2,3},{4,5},{6,7},{8,9},{10,11},{12,13},{14,15},{16,17},{18,... | collective-permute-start | bytes 786440 | tf_op jit(solution)/shard_map/ppermute | solution.py:30
  22.1 0.0 copy-done
  22.1 1.3 %fusion.11 = f32[4,2,128,256]{3,2,1,0:T(8,128)S(1)} fusion(bf16[1,4,2,256,256]{4,3,2,1,0:T(8,128)(2,1)S(1)} %copy-done, bf16[1,4,2,128,256]{4,3,2,1,0:T(8,128)(2,1)} %param.10), kind=kOutput, calls=%fused_computation.13 | convolution fusion | flops 134217728 | bytes 2621440 | tf_op jit(solution)/shard_map/bqrs,bqst->bqrt/dot_general | solution.py:34
  23.4 0.0 copy-done.7
  23.4 0.1 copy.12
  23.5 74.9 %shard_map.104 = bf16[16,64,256]{2,1,0:T(8,128)(2,1)} custom-call(bf16[16,64,256]{2,1,0:T(8,128)(2,1)} %bitcast.46, bf16[8,256,256]{2,1,0:T(8,128)(2,1)} %bitcast.42, bf16[8,256,256]{2,1,0:T(8,128)(2,1)} %bitcast.43, bf16[8,256,256]{2,1,0:T(8,128)(2,1)} %bitcast.45), custom_call_target="tpu_custom_call" | custom-call | flops 268435456 | bytes 4194304 | tf_op jit(solution)/shard_map/pallas_call | solution.py:166
  98.4 0.1 compare_bitcast_fusion
  98.5 0.0 collective-permute-done.2
  98.5 2.6 %fusion.7 = f32[4,2,128,256]{3,2,1,0:T(8,128)} fusion(bf16[1,4,2,256,256]{4,3,2,1,0:T(8,128)(2,1)} %param.15, bf16[4,1,128,256]{3,2,1,0:T(8,128)(2,1)S(1)} %get-tuple-element.3, bf16[4,1,128,256]{3,2,1,0:T(8,128)(2,1)} %collective-permute-done.2), kind=kOutput, calls=%fused_computation.9 | convolution fusion | flops 134479872 | bytes 2621440 | tf_op jit(solution)/shard_map/bqrs,bqst->bqrt/dot_general | solution.py:34
  101.1 0.0 collective-permute-done
  101.1 0.0 copy-done.1
  101.2 2.3 %convolution_add_fusion.1 = f32[4,2,128,256]{3,2,1,0:T(8,128)} fusion(f32[4,2,128,256]{3,2,1,0:T(8,128)S(1)} %fusion.11, bf16[1,4,2,256,256]{4,3,2,1,0:T(8,128)(2,1)S(1)} %copy-done.1, bf16[1,4,2,128,256]{4,3,2,1,0:T(8,128)(2,1)} %collective-permute-done), kind=kOutput, calls=%fused_computation.6 | convolution fusion | flops 134479872 | bytes 3670016 | tf_op jit(solution)/shard_map/bqrs,bqst->bqrt/dot_general | solution.py:34
  103.5 0.0 copy-start.2
  103.5 0.0 copy-start.3
  103.5 0.0 all-gather.3.cloned.1.call-done
  103.5 0.0 copy-start.6
  103.5 0.0 copy-start.4
  103.5 4.8 %fusion = bf16[2,4,128,256]{3,1,2,0:T(4,128)(2,1)S(1)} fusion(bf16[32,2,128,256]{3,2,1,0:T(8,128)(2,1)} %bitcast.41, pred[4,2,32,1]{2,1,0,3:T(4,128)(4,1)S(1)} %compare_bitcast_fusion), kind=kOutput, calls=%fused_computation | convolution fusion | flops 16777216 | bytes 4718848 | tf_op jit(solution)/shard_map/pqc,cqrs->pqrs/dot_general | solution.py:222
  108.3 0.0 copy-done.6
  108.3 0.0 copy-start.5
  108.3 0.3 fusion.5
  108.6 0.0 collective-permute-done.1
  108.6 0.0 copy-done.2
  108.6 0.0 copy-done.3
  108.6 0.0 copy-done.4
  108.7 2.4 %fusion.4 = f32[1,4,2,128,256]{4,3,2,1,0:T(8,128)} fusion(f32[4,2,128,256]{3,2,1,0:T(8,128)S(1)} %fusion.5, f32[4,2,128,256]{3,2,1,0:T(8,128)S(1)} %copy-done.3, f32[4,2,128,256]{3,2,1,0:T(8,128)S(1)} %copy-done.2, bf16[1,4,2,256,256]{4,3,2,1,0:T(8,128)(2,1)S(1)} %copy-done.4, bf16[1,4,2,128,256]{4,3,2,1,0:T(8,128)(2,1)} %collective-permute-done.1), kind=kOutput, calls=%fused_computation.5 | convolution fusion | flops 135004160 | bytes 5767168 | tf_op jit(solution)/shard_map/bqrs,bqst->bqrt/dot_general | solution.py:34
  111.0 0.0 copy-done.5
  111.0 0.8 copy.26
Async XLA Ops:
  7.2 14.9 %copy-start = (bf16[1,4,2,256,256]{4,3,2,1,0:T(8,128)(2,1)S(1)}, bf16[1,4,2,256,256]{4,3,2,1,0:T(8,128)(2,1)}, u32[]{:S(2)}) copy-start(bf16[1,4,2,256,256]{4,3,2,1,0:T(8,128)(2,1)} %param.11) | copy-start | bytes 3145732
  7.2 16.2 %copy-start.7 = (s32[1,4,2]{1,2,0:T(2,128)S(1)}, s32[1,4,2]{1,2,0:T(2,128)}, u32[]{:S(2)}) copy-start(s32[1,4,2]{1,2,0:T(2,128)} %param.17) | copy-start | bytes 100
  7.2 96.3 %all-gather.3.cloned.1.call-start = ((), (), s32[]{:S(2)}) async-start(), calls=%async_computation | async-start | bytes 4718592 | tf_op jit(solution)/shard_map/all_gather | solution.py:218
  7.9 100.7 %collective-permute-start.1 = (bf16[1,4,2,128,256]{4,3,2,1,0:T(8,128)(2,1)}, bf16[1,4,2,128,256]{4,3,2,1,0:T(8,128)(2,1)}, u32[]{:S(2)}, u32[]{:S(2)}) collective-permute-start(bf16[1,4,2,128,256]{4,3,2,1,0:T(8,128)(2,1)} %param.10), channel_id=1, source_target_pairs={{16,0},{32,16},{48,32},{64,48},{80,64},{96,80},{112,96},{128,112},... | collective-permute-start | bytes 1572872 | tf_op jit(solution)/shard_map/ppermute | solution.py:22
  13.1 88.1 %collective-permute-start = (bf16[1,4,2,128,256]{4,3,2,1,0:T(8,128)(2,1)}, bf16[1,4,2,128,256]{4,3,2,1,0:T(8,128)(2,1)}, u32[]{:S(2)}, u32[]{:S(2)}) collective-permute-start(bf16[1,4,2,128,256]{4,3,2,1,0:T(8,128)(2,1)} %param.10), channel_id=1, source_target_pairs={{0,16},{16,32},{32,48},{48,64},{64,80},{80,96},{96,112},{112,128},... | collective-permute-start | bytes 1572872 | tf_op jit(solution)/shard_map/ppermute | solution.py:19
  16.8 84.4 %copy-start.1 = (bf16[1,4,2,256,256]{4,3,2,1,0:T(8,128)(2,1)S(1)}, bf16[1,4,2,256,256]{4,3,2,1,0:T(8,128)(2,1)}, u32[]{:S(2)}) copy-start(bf16[1,4,2,256,256]{4,3,2,1,0:T(8,128)(2,1)} %param.12) | copy-start | bytes 3145732
  16.8 81.7 %collective-permute-start.2 = (bf16[4,1,128,256]{3,2,1,0:T(8,128)(2,1)}, bf16[4,1,128,256]{3,2,1,0:T(8,128)(2,1)}, u32[]{:S(2)}, u32[]{:S(2)}) collective-permute-start(bf16[4,1,128,256]{3,2,1,0:T(8,128)(2,1)} %get-tuple-element.2), channel_id=1, source_target_pairs={{0,1},{2,3},{4,5},{6,7},{8,9},{10,11},{12,13},{14,15},{16,17},{18,... | collective-permute-start | bytes 786440 | tf_op jit(solution)/shard_map/ppermute | solution.py:30
  103.5 5.1 %copy-start.2 = (f32[4,2,128,256]{3,2,1,0:T(8,128)S(1)}, f32[4,2,128,256]{3,2,1,0:T(8,128)}, u32[]{:S(2)}) copy-start(f32[4,2,128,256]{3,2,1,0:T(8,128)} %convolution_add_fusion.1) | copy-start | bytes 3145732
  103.5 5.2 %copy-start.3 = (f32[4,2,128,256]{3,2,1,0:T(8,128)S(1)}, f32[4,2,128,256]{3,2,1,0:T(8,128)}, u32[]{:S(2)}) copy-start(f32[4,2,128,256]{3,2,1,0:T(8,128)} %fusion.7) | copy-start | bytes 3145732
  103.5 4.8 %copy-start.6 = (bf16[1,4,2,256,256]{4,3,2,1,0:T(8,128)(2,1)S(1)}, bf16[1,4,2,256,256]{4,3,2,1,0:T(8,128)(2,1)}, u32[]{:S(2)}) copy-start(bf16[1,4,2,256,256]{4,3,2,1,0:T(8,128)(2,1)} %param.16) | copy-start | bytes 3145732
  103.5 5.2 %copy-start.4 = (bf16[1,4,2,256,256]{4,3,2,1,0:T(8,128)(2,1)S(1)}, bf16[1,4,2,256,256]{4,3,2,1,0:T(8,128)(2,1)}, u32[]{:S(2)}) copy-start(bf16[1,4,2,256,256]{4,3,2,1,0:T(8,128)(2,1)} %param.13) | copy-start | bytes 3145732
  108.3 2.7 %copy-start.5 = (bf16[16,64,256]{2,1,0:T(8,128)(2,1)S(1)}, bf16[16,64,256]{2,1,0:T(8,128)(2,1)}, u32[]{:S(2)}) copy-start(bf16[16,64,256]{2,1,0:T(8,128)(2,1)} %shard_map.104) | copy-start | bytes 1572868
Sparse Core Ops, SparseCore 0:
  9.8 61.2 all-gather.2

commit v2 on v1

v2 whole, which is shorter than its diff:
```python
import functools

import jax
import jax.numpy as jnp
from jax import lax
from jax.experimental import pallas as pl
from jax.experimental.pallas import tpu as pltpu
from jax.sharding import PartitionSpec as P

MESH = pl.DeviceIdType.MESH
ROW_SPLIT = 2


def apply_blocks(vectors, blocks):
    return jnp.einsum("bqrs,bqst->bqrt", vectors, blocks, preferred_element_type=jnp.float32)


def sweep_kernel(
    resid_ref,
    dir_ref,
    diag_ref,
    lower_ref,
    upper_ref,
    pivot_ref,
    downc_ref,
    out_ref,
    img_ref,
    fronts,
    fwd_buf,
    bwd_buf,
    below_buf,
    above_buf,
    rim_buf,
    fsend,
    frecv,
    bsend,
    brecv,
    hsend,
    hrecv,
    rsend,
    rrecv,
    *,
    n,
    nd,
    dc,
    per_block,
):
    f32 = jnp.float32
    bf16 = jnp.bfloat16
    h = lax.axis_index("elev")
    v = lax.axis_index("valley")
    d = lax.axis_index("down")
    chunks = resid_ref.shape[0]
    blocks = dir_ref.shape[0]
    rims = rim_buf.shape[0]
    has_below = h > 0
    has_above = h < n - 1
    has_up = d > 0
    has_dn = d < nd - 1

    barrier = pltpu.get_barrier_semaphore()
    peers = [
        (has_below, (h - 1, v, d)),
        (has_above, (h + 1, v, d)),
        (has_up, (h, v, d - 1)),
        (has_dn, (h, v, d + 1)),
    ]
    count = 0
    for cond, peer in peers:
        count = count + cond.astype(jnp.int32)

        @pl.when(cond)
        def _():
            pl.semaphore_signal(barrier, 1, device_id=peer, device_id_type=MESH)

    pl.semaphore_wait(barrier, count)

    def fwd_copy(g):
        return pltpu.make_async_remote_copy(
            src_ref=fronts.at[g],
            dst_ref=fwd_buf.at[g],
            send_sem=fsend.at[g],
            recv_sem=frecv.at[g],
            device_id=(h + 1, v, d),
            device_id_type=MESH,
        )

    def bwd_copy(g, src):
        return pltpu.make_async_remote_copy(
            src_ref=src.at[g],
            dst_ref=bwd_buf.at[g],
            send_sem=bsend.at[g],
            recv_sem=brecv.at[g],
            device_id=(h - 1, v, d),
            device_id_type=MESH,
        )

    def halo_down():
        return pltpu.make_async_remote_copy(
            src_ref=dir_ref,
            dst_ref=above_buf,
            send_sem=hsend.at[0],
            recv_sem=hrecv.at[0],
            device_id=(h - 1, v, d),
            device_id_type=MESH,
        )

    def halo_up():
        return pltpu.make_async_remote_copy(
            src_ref=dir_ref,
            dst_ref=below_buf,
            send_sem=hsend.at[1],
            recv_sem=hrecv.at[1],
            device_id=(h + 1, v, d),
            device_id_type=MESH,
        )

    def rim_copy(a):
        return pltpu.make_async_remote_copy(
            src_ref=dir_ref.at[a * dc + dc - 1],
            dst_ref=rim_buf.at[a],
            send_sem=rsend.at[a],
            recv_sem=rrecv.at[a],
            device_id=(h, v, d + 1),
            device_id_type=MESH,
        )

    @pl.when(has_below)
    def _():
        halo_down().start()

    @pl.when(has_dn)
    def _():
        for a in range(rims):
            rim_copy(a).start()

    @pl.when(jnp.logical_not(has_below))
    def _():
        below_buf[...] = jnp.zeros(below_buf.shape, bf16)

    @pl.when(jnp.logical_not(has_above))
    def _():
        above_buf[...] = jnp.zeros(above_buf.shape, bf16)

    @pl.when(jnp.logical_not(has_up))
    def _():
        rim_buf[...] = jnp.zeros(rim_buf.shape, bf16)

    def fwd_body(g, carry):
        blk = g // per_block

        @pl.when(has_below)
        def _():
            fwd_copy(g).wait_recv()
            inner = resid_ref[g].astype(f32) - jnp.dot(
                fwd_buf[g], lower_ref[blk], preferred_element_type=f32
            )
            fronts[g] = jnp.dot(
                inner.astype(bf16), pivot_ref[blk], preferred_element_type=f32
            ).astype(bf16)

        @pl.when(jnp.logical_not(has_below))
        def _():
            fronts[g] = jnp.dot(resid_ref[g], pivot_ref[blk], preferred_element_type=f32).astype(
                bf16
            )

        @pl.when(has_above)
        def _():
            fwd_copy(g).start()

        @pl.when(jnp.logical_not(has_above))
        def _():
            out_ref[g] = fronts[g]

        @pl.when(jnp.logical_and(jnp.logical_not(has_above), has_below))
        def _():
            bwd_copy(g, fronts).start()

        return carry

    lax.fori_loop(0, chunks, fwd_body, 0)

    @pl.when(has_above)
    def _():
        halo_up().start()

    def image_body(b, carry):
        a = b // dc
        c = b % dc
        acc = jnp.dot(dir_ref[b], diag_ref[b], preferred_element_type=f32)
        acc = acc + jnp.dot(below_buf[b], lower_ref[b], preferred_element_type=f32)
        acc = acc + jnp.dot(above_buf[b], upper_ref[b], preferred_element_type=f32)
        upstream = jnp.where(c == 0, rim_buf[a], dir_ref[jnp.maximum(b - 1, 0)])
        img_ref[b] = acc + jnp.dot(upstream, downc_ref[b], preferred_element_type=f32)
        return carry

    def image():
        @pl.when(has_below)
        def _():
            halo_up().wait_recv()

        @pl.when(has_above)
        def _():
            halo_down().wait_recv()

        @pl.when(has_up)
        def _():
            for a in range(rims):
                rim_copy(a).wait_recv()

        lax.fori_loop(0, blocks, image_body, 0)

    early = h < n // 2

    @pl.when(early)
    def _():
        image()

    def bwd_body(g, carry):
        blk = g // per_block

        @pl.when(has_above)
        def _():
            bwd_copy(g, out_ref).wait_recv()
            carried = jnp.dot(bwd_buf[g], upper_ref[blk], preferred_element_type=f32).astype(bf16)
            out_ref[g] = (
                fronts[g].astype(f32) - jnp.dot(carried, pivot_ref[blk], preferred_element_type=f32)
            ).astype(bf16)

            @pl.when(has_below)
            def _():
                bwd_copy(g, out_ref).start()

        return carry

    lax.fori_loop(0, chunks, bwd_body, 0)

    @pl.when(jnp.logical_not(early))
    def _():
        image()

    def drain(g, carry):
        @pl.when(has_above)
        def _():
            fwd_copy(g).wait_send()

        @pl.when(has_below)
        def _():
            bwd_copy(g, out_ref).wait_send()

        return carry

    lax.fori_loop(0, chunks, drain, 0)

    @pl.when(has_below)
    def _():
        halo_down().wait_send()

    @pl.when(has_above)
    def _():
        halo_up().wait_send()

    @pl.when(has_dn)
    def _():
        for a in range(rims):
            rim_copy(a).wait_send()


def sweep(resid_l, dir_l, diag_l, lower_l, upper_l, pivot_l, downc_l, dc):
    n = lax.axis_size("elev")
    nd = lax.axis_size("down")
    chunks, rows, width = resid_l.shape
    blocks = lower_l.shape[0]
    per_block = chunks // blocks
    vmem = pl.BlockSpec(memory_space=pltpu.VMEM)
    flops = 2 * (2 * chunks * rows + 4 * dir_l.shape[0] * dir_l.shape[1]) * width * width
    weight_bytes = 6 * lower_l.size * lower_l.dtype.itemsize
    return pl.pallas_call(
        functools.partial(sweep_kernel, n=n, nd=nd, dc=dc, per_block=per_block),
        out_shape=(
            jax.ShapeDtypeStruct(resid_l.shape, resid_l.dtype),
            jax.ShapeDtypeStruct(dir_l.shape, jnp.float32),
        ),
        in_specs=[vmem] * 7,
        out_specs=(vmem, vmem),
        scratch_shapes=[
            pltpu.VMEM(resid_l.shape, resid_l.dtype),
            pltpu.VMEM(resid_l.shape, resid_l.dtype),
            pltpu.VMEM(resid_l.shape, resid_l.dtype),
            pltpu.VMEM(dir_l.shape, dir_l.dtype),
            pltpu.VMEM(dir_l.shape, dir_l.dtype),
            pltpu.VMEM((blocks // dc,) + dir_l.shape[1:], dir_l.dtype),
            pltpu.SemaphoreType.DMA((chunks,)),
            pltpu.SemaphoreType.DMA((chunks,)),
            pltpu.SemaphoreType.DMA((chunks,)),
            pltpu.SemaphoreType.DMA((chunks,)),
            pltpu.SemaphoreType.DMA((2,)),
            pltpu.SemaphoreType.DMA((2,)),
            pltpu.SemaphoreType.DMA((blocks // dc,)),
            pltpu.SemaphoreType.DMA((blocks // dc,)),
        ],
        compiler_params=pltpu.CompilerParams(collective_id=0, has_side_effects=True),
        cost_estimate=pl.CostEstimate(
            flops=flops, bytes_accessed=weight_bytes + 6 * resid_l.size * 2, transcendentals=0
        ),
    )(resid_l, dir_l, diag_l, lower_l, upper_l, pivot_l, downc_l)


def local(
    resid,
    direction,
    diag_blocks,
    lower_blocks,
    upper_blocks,
    inv_pivots,
    down_coupling,
    valley_coupling,
    coupled_column,
):
    va, dc, nr, bs = resid.shape[1:]
    blocks = va * dc
    chunk_shape = (blocks * ROW_SPLIT, nr // ROW_SPLIT, bs)
    flat = (blocks, bs, bs)
    solved, partial = sweep(
        resid[0].reshape(chunk_shape),
        direction[0].reshape(blocks, nr, bs),
        diag_blocks[0].reshape(flat),
        lower_blocks[0].reshape(flat),
        upper_blocks[0].reshape(flat),
        inv_pivots[0].reshape(flat),
        down_coupling[0].reshape(flat),
        dc,
    )

    current = direction[0]
    partner_index = coupled_column[0]
    piece = lax.all_gather(current, "valley", axis=0, tiled=True)
    count = piece.shape[0]
    columns = jnp.arange(count, dtype=jnp.int32)
    picker = (partner_index[:, :, None] == columns[None, None, :]).astype(jnp.bfloat16)
    partner_sum = jnp.einsum("pqc,cqrs->pqrs", picker, piece, preferred_element_type=jnp.float32)
    partner = partner_sum.astype(jnp.bfloat16)
    total = partial.reshape(current.shape) + apply_blocks(partner, valley_coupling[0])
    return (solved.reshape(resid.shape), total[None])


def solution(mesh):
    spec = P("elev", "valley", "down", None, None)
    in_specs = (spec,) * 8 + (P("elev", "valley", "down"),)
    out_specs = (spec, spec)
    return jax.shard_map(local, mesh=mesh, in_specs=in_specs, out_specs=out_specs, check_vma=False)
```

time: 119 us -> 101 us (0.85)
  starting transfers between devices: 12.4 us -> 0.04 us
  matrix products: 13.8 us -> 6.02 us
  Pallas kernels: 74.9 us -> 78.2 us
    ppermute x3 -> x0, starting transfers between devices: 12.4 us -> none  [the longest x1 5.28 us: from_behind(): return lax.ppermute(value, axis, pairs)]
    dot_general x5 -> x1, matrix products: 8.96 us -> 1.29 us  [apply_blocks(): jnp.einsum('bqrs,bqst->bqrt', vectors, blocks, preferred_element_type=jnp...]
    pallas_call x1, Pallas kernels: 74.9 us -> 78.2 us  [sweep(): pl.pallas_call(functools.partial(sweep_kernel, n=n, nd=nd, dc=dc, per_blo...]
    slice x1 -> x0, local copies, waits for them, and re-layouts: 1.77 us -> none  [local(): rim_blocks = from_behind(current[:, -1:], 'down', 1)]
  transfers between devices with their start and end apart: 4 -> 1, of which waited for: 0 -> 0; matrix products, arithmetic and copies ran while one was open for 11% -> 1% of each run, Pallas kernels for 63% -> 78%
where the time goes in v2:
time: 101 us
  Pallas kernels  78.2 us (77%)
  between operations  14.1 us (14%)
  matrix products  6.02 us (6%)
  local copies, waits for them, and re-layouts  1.58 us (2%)
    pallas_call x1, Pallas kernels, sweep(): pl.pallas_call(functools.partial(sweep_kernel, n=n, nd=nd, dc=dc, per_blo...  78.2 us
    dot_general x1, matrix products, local(): jnp.einsum('pqc,cqrs->pqrs', picker, piece, preferred_element_type=jnp.fl...  4.73 us
  transfers between devices with their start and end apart: 1, of which 0 were waited for; matrix products, arithmetic and copies ran while one was open for 1% of the time, Pallas kernels for 78%

profile of v2, /device:TPU:1, one launch (start us, length us, event | category | flops | bytes accessed | tf_op | source)
XLA Modules:
  0.0 100.6 jit_solution(1711635591703030326)
XLA Ops:
  7.2 0.0 copy-start
  7.2 0.0 all-gather.3.cloned.1.call-start
  7.2 0.7 all-gather.3.cloned.1.call-update
  7.9 0.8 copy.12
  8.7 78.2 %shard_map.104 = (bf16[16,64,256]{2,1,0:T(8,128)(2,1)}, f32[8,128,256]{2,1,0:T(8,128)}) custom-call(bf16[16,64,256]{2,1,0:T(8,128)(2,1)} %bitcast.31, bf16[8,128,256]{2,1,0:T(8,128)(2,1)} %bitcast.24, bf16[8,256,256]{2,1,0:T(8,128)(2,1)} %bitcast.26, bf16[8,256,256]{2,1,0:T(8,128)(2,1)} %bitcast.27, bf16[8,256,256]{2,1,0:T(8,128)(2,1)} %bitcast.28, ...), custom_call_target="tpu_custom_call" | custom-call | flops 805306368 | bytes 9437184 | tf_op jit(solution)/shard_map/pallas_call | solution.py:279
  86.9 0.0 copy-start.1
  86.9 0.1 compare_bitcast_fusion
  86.9 0.0 all-gather.3.cloned.1.call-done
  87.0 0.0 copy-start.2
  87.0 4.7 %fusion = bf16[2,4,128,256]{3,1,2,0:T(4,128)(2,1)S(1)} fusion(bf16[32,2,128,256]{3,2,1,0:T(8,128)(2,1)} %bitcast.22, pred[4,2,32,1]{2,1,0,3:T(4,128)(4,1)S(1)} %compare_bitcast_fusion), kind=kOutput, calls=%fused_computation | convolution fusion | flops 16777216 | bytes 4718848 | tf_op jit(solution)/shard_map/pqc,cqrs->pqrs/dot_general | solution.py:342
  91.7 0.0 copy-done
  91.7 0.0 copy-done.1
  91.7 1.3 %fusion.2 = f32[1,4,2,128,256]{4,3,2,1,0:T(8,128)} fusion(f32[4,2,128,256]{3,2,1,0:T(8,128)S(1)} %bitcast.25, bf16[1,4,2,256,256]{4,3,2,1,0:T(8,128)(2,1)S(1)} %copy-done, bf16[2,4,128,256]{3,1,2,0:T(4,128)(2,1)S(1)} %fusion), kind=kOutput, calls=%fused_computation.3 | convolution fusion | flops 134479872 | bytes 3670016 | tf_op jit(solution)/shard_map/bqrs,bqst->bqrt/dot_general | solution.py:15
  93.0 0.0 copy-done.2
  93.0 0.8 copy.26
Async XLA Ops:
  7.2 84.5 %copy-start = (bf16[1,4,2,256,256]{4,3,2,1,0:T(8,128)(2,1)S(1)}, bf16[1,4,2,256,256]{4,3,2,1,0:T(8,128)(2,1)}, u32[]{:S(2)}) copy-start(bf16[1,4,2,256,256]{4,3,2,1,0:T(8,128)(2,1)} %param.16) | copy-start | bytes 3145732
  7.2 79.8 %all-gather.3.cloned.1.call-start = ((), (), s32[]{:S(2)}) async-start(), calls=%async_computation | async-start | bytes 4718592 | tf_op jit(solution)/shard_map/all_gather | solution.py:338
  86.9 4.8 %copy-start.1 = (f32[8,128,256]{2,1,0:T(8,128)S(1)}, f32[8,128,256]{2,1,0:T(8,128)}, u32[]{:S(2)}) copy-start(f32[8,128,256]{2,1,0:T(8,128)} %get-tuple-element.5) | copy-start | bytes 3145732
  87.0 6.0 %copy-start.2 = (bf16[16,64,256]{2,1,0:T(8,128)(2,1)S(1)}, bf16[16,64,256]{2,1,0:T(8,128)(2,1)}, u32[]{:S(2)}) copy-start(bf16[16,64,256]{2,1,0:T(8,128)(2,1)} %get-tuple-element.4) | copy-start | bytes 1572868
Sparse Core Ops, SparseCore 0:
  9.8 58.9 all-gather.2

commit v3 on v2

--- a/solution.py
+++ b/solution.py
@@ -9,10 +9,6 @@
 
 MESH = pl.DeviceIdType.MESH
 ROW_SPLIT = 2
-
-
-def apply_blocks(vectors, blocks):
-    return jnp.einsum("bqrs,bqst->bqrt", vectors, blocks, preferred_element_type=jnp.float32)
 
 
 def sweep_kernel(
@@ -23,6 +19,8 @@
     upper_ref,
     pivot_ref,
     downc_ref,
+    valc_ref,
+    col_ref,
     out_ref,
     img_ref,
     fronts,
@@ -31,6 +29,7 @@
     below_buf,
     above_buf,
     rim_buf,
+    gath,
     fsend,
     frecv,
     bsend,
@@ -39,8 +38,11 @@
     hrecv,
     rsend,
     rrecv,
+    gsend,
+    grecv,
     *,
     n,
+    nv,
     nd,
     dc,
     per_block,
@@ -53,6 +55,7 @@
     chunks = resid_ref.shape[0]
     blocks = dir_ref.shape[0]
     rims = rim_buf.shape[0]
+    va = blocks // dc
     has_below = h > 0
     has_above = h < n - 1
     has_up = d > 0
@@ -64,7 +67,7 @@
         (has_above, (h + 1, v, d)),
         (has_up, (h, v, d - 1)),
         (has_dn, (h, v, d + 1)),
-    ]
+    ] + [(v != p, (h, p, d)) for p in range(nv)]
     count = 0
     for cond, peer in peers:
         count = count + cond.astype(jnp.int32)
@@ -124,6 +127,34 @@
             device_id=(h, v, d + 1),
             device_id_type=MESH,
         )
+
+    def gather_copy(p):
+        return pltpu.make_async_remote_copy(
+            src_ref=dir_ref,
+            dst_ref=gath.at[pl.ds(v * blocks, blocks)],
+            send_sem=gsend.at[p],
+            recv_sem=grecv.at[v],
+            device_id=(h, p, d),
+            device_id_type=MESH,
+        )
+
+    def gather_wait(p):
+        return pltpu.make_async_remote_copy(
+            src_ref=dir_ref,
+            dst_ref=gath.at[pl.ds(p * blocks, blocks)],
+            send_sem=gsend.at[p],
+            recv_sem=grecv.at[p],
+            device_id=(h, p, d),
+            device_id_type=MESH,
+        )
+
+    for p in range(nv):
+
+        @pl.when(v != p)
+        def _():
+            gather_copy(p).start()
+
+    gath[pl.ds(v * blocks, blocks)] = dir_ref[...]
 
     @pl.when(has_below)
     def _():
@@ -192,7 +223,10 @@
         acc = acc + jnp.dot(below_buf[b], lower_ref[b], preferred_element_type=f32)
         acc = acc + jnp.dot(above_buf[b], upper_ref[b], preferred_element_type=f32)
         upstream = jnp.where(c == 0, rim_buf[a], dir_ref[jnp.maximum(b - 1, 0)])
-        img_ref[b] = acc + jnp.dot(upstream, downc_ref[b], preferred_element_type=f32)
+        acc = acc + jnp.dot(upstream, downc_ref[b], preferred_element_type=f32)
+        col = col_ref[b]
+        partner = gath[(col // va) * blocks + (col % va) * dc + c]
+        img_ref[b] = acc + jnp.dot(partner, valc_ref[b], preferred_element_type=f32)
         return carry
 
     def image():
@@ -208,6 +242,12 @@
         def _():
             for a in range(rims):
                 rim_copy(a).wait_recv()
+
+        for p in range(nv):
+
+            @pl.when(v != p)
+            def _():
+                gather_wait(p).wait_recv()
 
         lax.fori_loop(0, blocks, image_body, 0)
 
@@ -266,23 +306,30 @@
         for a in range(rims):
             rim_copy(a).wait_send()
 
-
-def sweep(resid_l, dir_l, diag_l, lower_l, upper_l, pivot_l, downc_l, dc):
+    for p in range(nv):
+
+        @pl.when(v != p)
+        def _():
+            gather_copy(p).wait_send()
+
+
+def sweep(resid_l, dir_l, diag_l, lower_l, upper_l, pivot_l, downc_l, valc_l, col_l, dc):
     n = lax.axis_size("elev")
+    nv = lax.axis_size("valley")
     nd = lax.axis_size("down")
     chunks, rows, width = resid_l.shape
     blocks = lower_l.shape[0]
     per_block = chunks // blocks
     vmem = pl.BlockSpec(memory_space=pltpu.VMEM)
-    flops = 2 * (2 * chunks * rows + 4 * dir_l.shape[0] * dir_l.shape[1]) * width * width
-    weight_bytes = 6 * lower_l.size * lower_l.dtype.itemsize
+    flops = 2 * (2 * chunks * rows + 5 * dir_l.shape[0] * dir_l.shape[1]) * width * width
+    weight_bytes = 7 * lower_l.size * lower_l.dtype.itemsize
     return pl.pallas_call(
-        functools.partial(sweep_kernel, n=n, nd=nd, dc=dc, per_block=per_block),
+        functools.partial(sweep_kernel, n=n, nv=nv, nd=nd, dc=dc, per_block=per_block),
         out_shape=(
             jax.ShapeDtypeStruct(resid_l.shape, resid_l.dtype),
             jax.ShapeDtypeStruct(dir_l.shape, jnp.float32),
         ),
-        in_specs=[vmem] * 7,
+        in_specs=[vmem] * 8 + [pl.BlockSpec(memory_space=pltpu.SMEM)],
         out_specs=(vmem, vmem),
         scratch_shapes=[
             pltpu.VMEM(resid_l.shape, resid_l.dtype),
@@ -291,6 +338,7 @@
             pltpu.VMEM(dir_l.shape, dir_l.dtype),
             pltpu.VMEM(dir_l.shape, dir_l.dtype),
             pltpu.VMEM((blocks // dc,) + dir_l.shape[1:], dir_l.dtype),
+            pltpu.VMEM((nv * blocks,) + dir_l.shape[1:], dir_l.dtype),
             pltpu.SemaphoreType.DMA((chunks,)),
             pltpu.SemaphoreType.DMA((chunks,)),
             pltpu.SemaphoreType.DMA((chunks,)),
@@ -299,12 +347,14 @@
             pltpu.SemaphoreType.DMA((2,)),
             pltpu.SemaphoreType.DMA((blocks // dc,)),
             pltpu.SemaphoreType.DMA((blocks // dc,)),
+            pltpu.SemaphoreType.DMA((nv,)),
+            pltpu.SemaphoreType.DMA((nv,)),
         ],
         compiler_params=pltpu.CompilerParams(collective_id=0, has_side_effects=True),
         cost_estimate=pl.CostEstimate(
             flops=flops, bytes_accessed=weight_bytes + 6 * resid_l.size * 2, transcendentals=0
         ),
-    )(resid_l, dir_l, diag_l, lower_l, upper_l, pivot_l, downc_l)
+    )(resid_l, dir_l, diag_l, lower_l, upper_l, pivot_l, downc_l, valc_l, col_l)
 
 
 def local(
@@ -322,7 +372,7 @@
     blocks = va * dc
     chunk_shape = (blocks * ROW_SPLIT, nr // ROW_SPLIT, bs)
     flat = (blocks, bs, bs)
-    solved, partial = sweep(
+    solved, image = sweep(
         resid[0].reshape(chunk_shape),
         direction[0].reshape(blocks, nr, bs),
         diag_blocks[0].reshape(flat),
@@ -330,19 +380,11 @@
         upper_blocks[0].reshape(flat),
         inv_pivots[0].reshape(flat),
         down_coupling[0].reshape(flat),
+        valley_coupling[0].reshape(flat),
+        coupled_column[0].reshape(blocks),
         dc,
     )
-
-    current = direction[0]
-    partner_index = coupled_column[0]
-    piece = lax.all_gather(current, "valley", axis=0, tiled=True)
-    count = piece.shape[0]
-    columns = jnp.arange(count, dtype=jnp.int32)
-    picker = (partner_index[:, :, None] == columns[None, None, :]).astype(jnp.bfloat16)
-    partner_sum = jnp.einsum("pqc,cqrs->pqrs", picker, piece, preferred_element_type=jnp.float32)
-    partner = partner_sum.astype(jnp.bfloat16)
-    total = partial.reshape(current.shape) + apply_blocks(partner, valley_coupling[0])
-    return (solved.reshape(resid.shape), total[None])
+    return (solved.reshape(resid.shape), image.reshape(resid.shape))
 
 
 def solution(mesh):

time: 101 us -> 107 us (1.059)
  the two profiles are of different devices: /device:TPU:1 before, /device:TPU:30 now
where the time goes in v3:
time: 107 us
  Pallas kernels  102 us (95%)
  local copies, waits for them, and re-layouts  4.29 us (4%)
    pallas_call x1, Pallas kernels, sweep(): pl.pallas_call(functools.partial(sweep_kernel, n=n, nv=nv, nd=nd, dc=dc,...  102 us
    unnamed x7, local copies, waits for them, and re-layouts  3.69 us

profile of v3, /device:TPU:30, one launch (start us, length us, event | category | flops | bytes accessed | tf_op | source)
XLA Modules:
  0.0 107.1 jit_solution(8903838957007889214)
XLA Ops:
  0.6 0.0 copy-start.1
  0.6 0.7 copy-done.1
  1.3 0.1 copy.12
  1.4 0.6 reshape_squeeze.35.col_ref
  2.0 102.2 %shard_map.104 = (bf16[16,64,256]{2,1,0:T(8,128)(2,1)}, f32[8,128,256]{2,1,0:T(8,128)}) custom-call(bf16[16,64,256]{2,1,0:T(8,128)(2,1)} %bitcast.18, bf16[8,128,256]{2,1,0:T(8,128)(2,1)} %bitcast.19, bf16[8,256,256]{2,1,0:T(8,128)(2,1)} %bitcast.11, bf16[8,256,256]{2,1,0:T(8,128)(2,1)} %bitcast.12, bf16[8,256,256]{2,1,0:T(8,128)(2,1)} %bitcast.13, ...), custom_call_target="tpu_custom_call" | custom-call | flops 939524096 | bytes 10485760 | tf_op jit(solution)/shard_map/pallas_call | solution.py:326
  104.2 0.0 copy-start
  104.2 2.0 %copy.15 = bf16[1,4,2,128,256]{4,3,2,1,0:T(8,128)(2,1)} copy(bf16[1,4,2,128,256]{4,3,2,1,0:T(8,128)(2,1)} %bitcast.17) | data formatting | bytes 1048576
  106.2 0.0 copy-done
  106.2 1.0 copy.16
Async XLA Ops:
  0.6 0.7 copy-start.1
  104.2 2.0 %copy-start = (f32[8,128,256]{2,1,0:T(8,128)S(1)}, f32[8,128,256]{2,1,0:T(8,128)}, u32[]{:S(2)}) copy-start(f32[8,128,256]{2,1,0:T(8,128)} %get-tuple-element.5) | copy-start | bytes 3145732

commit v4 on v3

--- a/solution.py
+++ b/solution.py
@@ -223,10 +223,14 @@
         acc = acc + jnp.dot(below_buf[b], lower_ref[b], preferred_element_type=f32)
         acc = acc + jnp.dot(above_buf[b], upper_ref[b], preferred_element_type=f32)
         upstream = jnp.where(c == 0, rim_buf[a], dir_ref[jnp.maximum(b - 1, 0)])
-        acc = acc + jnp.dot(upstream, downc_ref[b], preferred_element_type=f32)
+        img_ref[b] = acc + jnp.dot(upstream, downc_ref[b], preferred_element_type=f32)
+        return carry
+
+    def partner_body(b, carry):
+        c = b % dc
         col = col_ref[b]
         partner = gath[(col // va) * blocks + (col % va) * dc + c]
-        img_ref[b] = acc + jnp.dot(partner, valc_ref[b], preferred_element_type=f32)
+        img_ref[b] = img_ref[b] + jnp.dot(partner, valc_ref[b], preferred_element_type=f32)
         return carry
 
     def image():
@@ -242,12 +246,6 @@
         def _():
             for a in range(rims):
                 rim_copy(a).wait_recv()
-
-        for p in range(nv):
-
-            @pl.when(v != p)
-            def _():
-                gather_wait(p).wait_recv()
 
         lax.fori_loop(0, blocks, image_body, 0)
 
@@ -279,6 +277,14 @@
     @pl.when(jnp.logical_not(early))
     def _():
         image()
+
+    for p in range(nv):
+
+        @pl.when(v != p)
+        def _():
+            gather_wait(p).wait_recv()
+
+    lax.fori_loop(0, blocks, partner_body, 0)
 
     def drain(g, carry):
         @pl.when(has_above)

time: 107 us -> 108 us (level)
    pallas_call x1, Pallas kernels: 102 us -> 103 us  [sweep(): pl.pallas_call(functools.partial(sweep_kernel, n=n, nv=nv, nd=nd, dc=dc,...]
where the time goes in v4:
time: 108 us
  Pallas kernels  103 us (95%)
  local copies, waits for them, and re-layouts  4.29 us (4%)
    pallas_call x1, Pallas kernels, sweep(): pl.pallas_call(functools.partial(sweep_kernel, n=n, nv=nv, nd=nd, dc=dc,...  103 us
    unnamed x7, local copies, waits for them, and re-layouts  3.69 us

profile of v4, /device:TPU:30, one launch (start us, length us, event | category | flops | bytes accessed | tf_op | source)
XLA Modules:
  0.0 108.3 jit_solution(10219438526167244078)
XLA Ops:
  0.6 0.0 copy-start.1
  0.6 0.7 copy-done.1
  1.3 0.1 copy.12
  1.4 0.6 reshape_squeeze.35.col_ref
  2.0 103.4 %shard_map.104 = (bf16[16,64,256]{2,1,0:T(8,128)(2,1)}, f32[8,128,256]{2,1,0:T(8,128)}) custom-call(bf16[16,64,256]{2,1,0:T(8,128)(2,1)} %bitcast.18, bf16[8,128,256]{2,1,0:T(8,128)(2,1)} %bitcast.19, bf16[8,256,256]{2,1,0:T(8,128)(2,1)} %bitcast.11, bf16[8,256,256]{2,1,0:T(8,128)(2,1)} %bitcast.12, bf16[8,256,256]{2,1,0:T(8,128)(2,1)} %bitcast.13, ...), custom_call_target="tpu_custom_call" | custom-call | flops 939524096 | bytes 10485760 | tf_op jit(solution)/shard_map/pallas_call | solution.py:332
  105.4 0.0 copy-start
  105.4 2.0 %copy.15 = bf16[1,4,2,128,256]{4,3,2,1,0:T(8,128)(2,1)} copy(bf16[1,4,2,128,256]{4,3,2,1,0:T(8,128)(2,1)} %bitcast.17) | data formatting | bytes 1048576
  107.3 0.0 copy-done
  107.3 1.0 copy.16
Async XLA Ops:
  0.6 0.7 copy-start.1
  105.4 2.0 %copy-start = (f32[8,128,256]{2,1,0:T(8,128)S(1)}, f32[8,128,256]{2,1,0:T(8,128)}, u32[]{:S(2)}) copy-start(f32[8,128,256]{2,1,0:T(8,128)} %get-tuple-element.5) | copy-start | bytes 3145732

commit v5 on v2

--- a/solution.py
+++ b/solution.py
@@ -8,7 +8,7 @@
 from jax.sharding import PartitionSpec as P
 
 MESH = pl.DeviceIdType.MESH
-ROW_SPLIT = 2
+ROW_SPLIT = 4
 
 
 def apply_blocks(vectors, blocks):
@@ -336,11 +336,10 @@
     current = direction[0]
     partner_index = coupled_column[0]
     piece = lax.all_gather(current, "valley", axis=0, tiled=True)
-    count = piece.shape[0]
-    columns = jnp.arange(count, dtype=jnp.int32)
-    picker = (partner_index[:, :, None] == columns[None, None, :]).astype(jnp.bfloat16)
-    partner_sum = jnp.einsum("pqc,cqrs->pqrs", picker, piece, preferred_element_type=jnp.float32)
-    partner = partner_sum.astype(jnp.bfloat16)
+    rows = partner_index * dc + jnp.arange(dc, dtype=jnp.int32)[None, :]
+    partner = jnp.take(
+        piece.reshape((-1,) + piece.shape[2:]), rows.reshape(-1), axis=0, mode="clip"
+    ).reshape(current.shape)
     total = partial.reshape(current.shape) + apply_blocks(partner, valley_coupling[0])
     return (solved.reshape(resid.shape), total[None])
 

time: 101 us -> 104 us (1.030)
  Pallas kernels: 78.2 us -> 82.1 us
  matrix products: 6.02 us -> 2.51 us
  local copies, waits for them, and re-layouts: 1.58 us -> 3.89 us
    dot_general x1 -> x0, matrix products: 4.73 us -> none  [local(): jnp.einsum('pqc,cqrs->pqrs', picker, piece, preferred_element_type=jnp.fl...]
    pallas_call x1, Pallas kernels: 78.2 us -> 82.1 us  [sweep(): pl.pallas_call(functools.partial(sweep_kernel, n=n, nd=nd, dc=dc, per_blo...]
    gather x0 -> x1, local copies, waits for them, and re-layouts: none -> 2.81 us  [local(): jnp.take(piece.reshape((-1,) + piece.shape[2:]), rows.reshape(-1), axis=0...]
    dot_general x1, matrix products: 1.29 us -> 2.51 us  [apply_blocks(): jnp.einsum('bqrs,bqst->bqrt', vectors, blocks, preferred_element_type=jnp...]
  transfers between devices with their start and end apart: 1 -> 1, of which waited for: 0 -> 0; matrix products, arithmetic and copies ran while one was open for 1% -> 1% of each run, Pallas kernels for 78% -> 79%
where the time goes in v5:
time: 104 us
  Pallas kernels  82.1 us (79%)
  between operations  14.1 us (14%)
  local copies, waits for them, and re-layouts  3.89 us (4%)
  matrix products  2.51 us (2%)
    pallas_call x1, Pallas kernels, sweep(): pl.pallas_call(functools.partial(sweep_kernel, n=n, nd=nd, dc=dc, per_blo...  82.1 us
    gather x1, local copies, waits for them, and re-layouts, local(): jnp.take(piece.reshape((-1,) + piece.shape[2:]), rows.reshape(-1), axis=0...  2.81 us
    dot_general x1, matrix products, apply_blocks(): jnp.einsum('bqrs,bqst->bqrt', vectors, blocks, preferred_element_type=jnp...  2.51 us
  transfers between devices with their start and end apart: 1, of which 0 were waited for; matrix products, arithmetic and copies ran while one was open for 1% of the time, Pallas kernels for 79%

profile of v5, /device:TPU:1, one launch (start us, length us, event | category | flops | bytes accessed | tf_op | source)
XLA Modules:
  0.0 104.0 jit_solution(11848157531423825856)
XLA Ops:
  7.2 0.0 copy-start
  7.2 0.0 all-gather.3.cloned.1.call-start
  7.2 0.7 all-gather.3.cloned.1.call-update
  7.9 0.7 broadcast_multiply_fusion
  8.6 0.1 copy.14
  8.7 0.1 mul.14
  8.8 0.1 add.21
  8.9 82.1 %shard_map.104 = (bf16[32,32,256]{2,1,0:T(8,128)(2,1)}, f32[8,128,256]{2,1,0:T(8,128)}) custom-call(bf16[32,32,256]{2,1,0:T(8,128)(2,1)} %bitcast.29, bf16[8,128,256]{2,1,0:T(8,128)(2,1)} %bitcast.21, bf16[8,256,256]{2,1,0:T(8,128)(2,1)} %bitcast.24, bf16[8,256,256]{2,1,0:T(8,128)(2,1)} %bitcast.25, bf16[8,256,256]{2,1,0:T(8,128)(2,1)} %bitcast.26, ...), custom_call_target="tpu_custom_call" | custom-call | flops 805306368 | bytes 9437184 | tf_op jit(solution)/shard_map/pallas_call | solution.py:279
  91.0 0.0 copy-start.1
  91.0 0.0 all-gather.3.cloned.1.call-done
  91.0 2.8 %gather_fusion = bf16[8,128,256]{2,1,0:T(8,128)(2,1)S(1)} fusion(bf16[64,128,256]{2,1,0:T(8,128)(2,1)} %bitcast.31, s32[1024]{0:T(1024)S(1)} %pad_clamp_fusion), kind=kCustom, calls=%fused_computation | custom fusion | bytes 1048608 | tf_op jit(solution)/shard_map/jit(_take)/gather | solution.py:340
  93.8 0.0 copy-done
  93.9 2.5 %fusion = f32[1,4,2,128,256]{4,3,2,1,0:T(8,128)} fusion(f32[4,2,128,256]{3,2,1,0:T(8,128)} %bitcast.23, bf16[4,2,128,256]{3,2,1,0:T(8,128)(2,1)S(1)} %bitcast.22, bf16[1,4,2,256,256]{4,3,2,1,0:T(8,128)(2,1)S(1)} %copy-done), kind=kOutput, calls=%fused_computation.2 | convolution fusion | flops 134479872 | bytes 3670016 | tf_op jit(solution)/shard_map/bqrs,bqst->bqrt/dot_general | solution.py:15
  96.4 0.0 copy-done.1
  96.4 0.8 copy.16
  (3 shorter events, 0.0 us)
Async XLA Ops:
  7.2 86.7 %copy-start = (bf16[1,4,2,256,256]{4,3,2,1,0:T(8,128)(2,1)S(1)}, bf16[1,4,2,256,256]{4,3,2,1,0:T(8,128)(2,1)}, u32[]{:S(2)}) copy-start(bf16[1,4,2,256,256]{4,3,2,1,0:T(8,128)(2,1)} %param.16) | copy-start | bytes 3145732
  7.2 83.8 %all-gather.3.cloned.1.call-start = ((), (), s32[]{:S(2)}) async-start(), calls=%async_computation | async-start | bytes 4718592 | tf_op jit(solution)/shard_map/all_gather | solution.py:338
  91.0 5.4 %copy-start.1 = (bf16[32,32,256]{2,1,0:T(8,128)(2,1)S(1)}, bf16[32,32,256]{2,1,0:T(8,128)(2,1)}, u32[]{:S(2)}) copy-start(bf16[32,32,256]{2,1,0:T(8,128)(2,1)} %get-tuple-element.4) | copy-start | bytes 1572868
Sparse Core Ops, SparseCore 0:
  9.8 58.9 all-gather.2

commit v6 on v2

--- a/solution.py
+++ b/solution.py
@@ -307,6 +307,36 @@
     )(resid_l, dir_l, diag_l, lower_l, upper_l, pivot_l, downc_l)
 
 
+def partner_kernel(col_ref, piece_ref, valc_ref, partial_ref, out_ref):
+    out_ref[...] = partial_ref[...] + jnp.dot(
+        piece_ref[0], valc_ref[0], preferred_element_type=jnp.float32
+    )[None]
+
+
+def add_partner(cols, piece, valc, partial, dc):
+    blocks, rows, width = partial.shape
+    spec = pl.BlockSpec((1, rows, width), lambda b, col: (b, 0, 0))
+    return pl.pallas_call(
+        partner_kernel,
+        out_shape=jax.ShapeDtypeStruct(partial.shape, partial.dtype),
+        grid_spec=pltpu.PrefetchScalarGridSpec(
+            num_scalar_prefetch=1,
+            grid=(blocks,),
+            in_specs=[
+                pl.BlockSpec((1, rows, width), lambda b, col: (col[b] * dc + b % dc, 0, 0)),
+                pl.BlockSpec((1, width, width), lambda b, col: (b, 0, 0)),
+                spec,
+            ],
+            out_specs=spec,
+        ),
+        cost_estimate=pl.CostEstimate(
+            flops=2 * blocks * rows * width * width,
+            bytes_accessed=blocks * (rows * width * 10 + width * width * 2),
+            transcendentals=0,
+        ),
+    )(cols, piece, valc, partial)
+
+
 def local(
     resid,
     direction,
@@ -334,15 +364,15 @@
     )
 
     current = direction[0]
-    partner_index = coupled_column[0]
     piece = lax.all_gather(current, "valley", axis=0, tiled=True)
-    count = piece.shape[0]
-    columns = jnp.arange(count, dtype=jnp.int32)
-    picker = (partner_index[:, :, None] == columns[None, None, :]).astype(jnp.bfloat16)
-    partner_sum = jnp.einsum("pqc,cqrs->pqrs", picker, piece, preferred_element_type=jnp.float32)
-    partner = partner_sum.astype(jnp.bfloat16)
-    total = partial.reshape(current.shape) + apply_blocks(partner, valley_coupling[0])
-    return (solved.reshape(resid.shape), total[None])
+    image = add_partner(
+        coupled_column[0].reshape(blocks),
+        piece.reshape((-1, nr, bs)),
+        valley_coupling[0].reshape(flat),
+        partial,
+        dc,
+    )
+    return (solved.reshape(resid.shape), image.reshape(resid.shape))
 
 
 def solution(mesh):

time: 101 us -> 102 us (level)
  Pallas kernels: 78.2 us -> 85.1 us
  matrix products: 6.02 us -> 0 us
    pallas_call x0 -> x1, Pallas kernels: none -> 6.76 us  [add_partner(): pl.pallas_call(partner_kernel, out_shape=jax.ShapeDtypeStruct(partial.sha...]
    dot_general x2 -> x0, matrix products: 6.02 us -> none  [the longest x1 4.73 us: local(): jnp.einsum('pqc,cqrs->pqrs', picker, piece, preferred_element_type=jnp.fl...]
  transfers between devices with their start and end apart: 1 -> 1, of which waited for: 0 -> 0; matrix products, arithmetic and copies ran while one was open for 1% -> 1% of each run, Pallas kernels for 78% -> 77%
where the time goes in v6:
time: 102 us; the launch traced here: 101 us
  Pallas kernels  85.1 us (83%)
  between operations  14.1 us (14%)
  local copies, waits for them, and re-layouts  1.49 us (1%)
    pallas_call x1, Pallas kernels, sweep(): pl.pallas_call(functools.partial(sweep_kernel, n=n, nd=nd, dc=dc, per_blo...  78.3 us
    pallas_call x1, Pallas kernels, add_partner(): pl.pallas_call(partner_kernel, out_shape=jax.ShapeDtypeStruct(partial.sha...  6.76 us
  transfers between devices with their start and end apart: 1, of which 0 were waited for; matrix products, arithmetic and copies ran while one was open for 1% of the time, Pallas kernels for 77%

profile of v6, /device:TPU:1, one launch (start us, length us, event | category | flops | bytes accessed | tf_op | source)
XLA Modules:
  0.0 101.3 jit_solution(15368207232310335690)
XLA Ops:
  7.2 0.0 copy-start.1
  7.2 0.0 all-gather.3.cloned.1.call-start
  7.2 0.7 all-gather.3.cloned.1.call-update
  7.9 78.3 %shard_map.104 = (bf16[16,64,256]{2,1,0:T(8,128)(2,1)}, f32[8,128,256]{2,1,0:T(8,128)}) custom-call(bf16[16,64,256]{2,1,0:T(8,128)(2,1)} %bitcast.22, bf16[8,128,256]{2,1,0:T(8,128)(2,1)} %bitcast.14, bf16[8,256,256]{2,1,0:T(8,128)(2,1)} %bitcast.15, bf16[8,256,256]{2,1,0:T(8,128)(2,1)} %bitcast.16, bf16[8,256,256]{2,1,0:T(8,128)(2,1)} %bitcast.17, ...), custom_call_target="tpu_custom_call" | custom-call | flops 805306368 | bytes 9437184 | tf_op jit(solution)/shard_map/pallas_call | solution.py:279
  86.2 0.0 copy-start
  86.2 0.0 copy-done.1
  86.3 0.1 copy.13
  86.3 0.6 reshape_squeeze.34.col_ref
  86.9 0.0 all-gather.3.cloned.1.call-done
  86.9 6.8 %shard_map.105 = f32[8,128,256]{2,1,0:T(8,128)} custom-call(s32[8]{0:T(128)} %reshape_squeeze.34.col_ref, bf16[64,128,256]{2,1,0:T(8,128)(2,1)} %bitcast.12, bf16[8,256,256]{2,1,0:T(8,128)(2,1)} %bitcast.20, f32[8,128,256]{2,1,0:T(8,128)} %get-tuple-element.5.partial_ref), custom_call_target="tpu_custom_call" | custom-call | flops 134217728 | bytes 3670016 | tf_op jit(solution)/shard_map/pallas_call | solution.py:319
  93.7 0.0 copy-done
  93.7 0.8 copy.16
Async XLA Ops:
  7.2 79.1 %copy-start.1 = (s32[1,4,2]{1,2,0:T(2,128)S(1)}, s32[1,4,2]{1,2,0:T(2,128)}, u32[]{:S(2)}) copy-start(s32[1,4,2]{1,2,0:T(2,128)} %param.17) | copy-start | bytes 100
  7.2 79.8 %all-gather.3.cloned.1.call-start = ((), (), s32[]{:S(2)}) async-start(), calls=%async_computation | async-start | bytes 4718592 | tf_op jit(solution)/shard_map/all_gather | solution.py:367
  86.2 7.5 %copy-start = (bf16[16,64,256]{2,1,0:T(8,128)(2,1)S(1)}, bf16[16,64,256]{2,1,0:T(8,128)(2,1)}, u32[]{:S(2)}) copy-start(bf16[16,64,256]{2,1,0:T(8,128)(2,1)} %get-tuple-element.4) | copy-start | bytes 1572868
Sparse Core Ops, SparseCore 0:
  9.8 59.1 all-gather.2

commit v7 on v6

--- a/solution.py
+++ b/solution.py
@@ -307,28 +307,38 @@
     )(resid_l, dir_l, diag_l, lower_l, upper_l, pivot_l, downc_l)
 
 
-def partner_kernel(col_ref, piece_ref, valc_ref, partial_ref, out_ref):
-    out_ref[...] = partial_ref[...] + jnp.dot(
-        piece_ref[0], valc_ref[0], preferred_element_type=jnp.float32
-    )[None]
+def partner_kernel(col_ref, piece_ref, valc_ref, partial_ref, out_ref, held, sems, *, dc):
+    blocks = held.shape[0]
+    copies = []
+    for b in range(blocks):
+        col = col_ref[0, b // dc, b % dc]
+        copy = pltpu.make_async_copy(piece_ref.at[col * dc + b % dc], held.at[b], sems.at[b])
+        copy.start()
+        copies.append(copy)
+    for b in range(blocks):
+        copies[b].wait()
+        out_ref[b] = partial_ref[b] + jnp.dot(
+            held[b], valc_ref[b], preferred_element_type=jnp.float32
+        )
 
 
 def add_partner(cols, piece, valc, partial, dc):
     blocks, rows, width = partial.shape
-    spec = pl.BlockSpec((1, rows, width), lambda b, col: (b, 0, 0))
+    vmem = pl.BlockSpec(memory_space=pltpu.VMEM)
     return pl.pallas_call(
-        partner_kernel,
+        functools.partial(partner_kernel, dc=dc),
         out_shape=jax.ShapeDtypeStruct(partial.shape, partial.dtype),
-        grid_spec=pltpu.PrefetchScalarGridSpec(
-            num_scalar_prefetch=1,
-            grid=(blocks,),
-            in_specs=[
-                pl.BlockSpec((1, rows, width), lambda b, col: (col[b] * dc + b % dc, 0, 0)),
-                pl.BlockSpec((1, width, width), lambda b, col: (b, 0, 0)),
-                spec,
-            ],
-            out_specs=spec,
-        ),
+        in_specs=[
+            pl.BlockSpec(memory_space=pltpu.SMEM),
+            pl.BlockSpec(memory_space=pl.ANY),
+            vmem,
+            vmem,
+        ],
+        out_specs=vmem,
+        scratch_shapes=[
+            pltpu.VMEM((blocks, rows, width), piece.dtype),
+            pltpu.SemaphoreType.DMA((blocks,)),
+        ],
         cost_estimate=pl.CostEstimate(
             flops=2 * blocks * rows * width * width,
             bytes_accessed=blocks * (rows * width * 10 + width * width * 2),
@@ -366,7 +376,7 @@
     current = direction[0]
     piece = lax.all_gather(current, "valley", axis=0, tiled=True)
     image = add_partner(
-        coupled_column[0].reshape(blocks),
+        coupled_column,
         piece.reshape((-1, nr, bs)),
         valley_coupling[0].reshape(flat),
         partial,

time: 102 us -> 99.6 us (0.976)
  Pallas kernels: 85.1 us -> 83.2 us
    pallas_call x1, Pallas kernels: 6.76 us -> 4.9 us  [add_partner(): pl.pallas_call(functools.partial(partner_kernel, dc=dc), out_shape=jax.Sh...]
  transfers between devices with their start and end apart: 1 -> 1, of which waited for: 0 -> 0; matrix products, arithmetic and copies ran while one was open for 1% -> 1% of each run, Pallas kernels for 77% -> 79%
where the time goes in v7:
time: 99.6 us; the launch traced here: 99.5 us
  Pallas kernels  83.2 us (84%)
  between operations  14.1 us (14%)
  local copies, waits for them, and re-layouts  1.47 us (1%)
    pallas_call x1, Pallas kernels, sweep(): pl.pallas_call(functools.partial(sweep_kernel, n=n, nd=nd, dc=dc, per_blo...  78.3 us
    pallas_call x1, Pallas kernels, add_partner(): pl.pallas_call(functools.partial(partner_kernel, dc=dc), out_shape=jax.Sh...  4.9 us
  transfers between devices with their start and end apart: 1, of which 0 were waited for; matrix products, arithmetic and copies ran while one was open for 1% of the time, Pallas kernels for 79%

profile of v7, /device:TPU:1, one launch (start us, length us, event | category | flops | bytes accessed | tf_op | source)
XLA Modules:
  0.0 99.5 jit_solution(6119133273851347602)
XLA Ops:
  7.2 0.0 copy-start.1
  7.2 0.0 all-gather.3.cloned.1.call-start
  7.2 0.7 all-gather.3.cloned.1.call-update
  7.9 78.3 %shard_map.104 = (bf16[16,64,256]{2,1,0:T(8,128)(2,1)}, f32[8,128,256]{2,1,0:T(8,128)}) custom-call(bf16[16,64,256]{2,1,0:T(8,128)(2,1)} %bitcast.22, bf16[8,128,256]{2,1,0:T(8,128)(2,1)} %bitcast.14, bf16[8,256,256]{2,1,0:T(8,128)(2,1)} %bitcast.15, bf16[8,256,256]{2,1,0:T(8,128)(2,1)} %bitcast.16, bf16[8,256,256]{2,1,0:T(8,128)(2,1)} %bitcast.17, ...), custom_call_target="tpu_custom_call" | custom-call | flops 805306368 | bytes 9437184 | tf_op jit(solution)/shard_map/pallas_call | solution.py:279
  86.2 0.0 copy-start
  86.2 0.0 copy-done.1
  86.3 0.7 copy.13.col_ref
  86.9 0.0 all-gather.3.cloned.1.call-done
  86.9 4.9 %shard_map.105 = f32[8,128,256]{2,1,0:T(8,128)} custom-call(s32[1,4,2]{2,1,0:T(4,128)} %copy.13.col_ref, bf16[64,128,256]{2,1,0:T(8,128)(2,1)} %bitcast.12, bf16[8,256,256]{2,1,0:T(8,128)(2,1)} %bitcast.20, f32[8,128,256]{2,1,0:T(8,128)} %get-tuple-element.5.partial_ref), custom_call_target="tpu_custom_call" | custom-call | flops 134217728 | bytes 3670016 | tf_op jit(solution)/shard_map/pallas_call | solution.py:328
  91.8 0.0 copy-done
  91.8 0.8 copy.15
Async XLA Ops:
  7.2 79.1 %copy-start.1 = (s32[1,4,2]{1,2,0:T(2,128)S(1)}, s32[1,4,2]{1,2,0:T(2,128)}, u32[]{:S(2)}) copy-start(s32[1,4,2]{1,2,0:T(2,128)} %param.17) | copy-start | bytes 100
  7.2 79.7 %all-gather.3.cloned.1.call-start = ((), (), s32[]{:S(2)}) async-start(), calls=%async_computation | async-start | bytes 4718592 | tf_op jit(solution)/shard_map/all_gather | solution.py:377
  86.2 5.6 %copy-start = (bf16[16,64,256]{2,1,0:T(8,128)(2,1)S(1)}, bf16[16,64,256]{2,1,0:T(8,128)(2,1)}, u32[]{:S(2)}) copy-start(bf16[16,64,256]{2,1,0:T(8,128)(2,1)} %get-tuple-element.4) | copy-start | bytes 1572868
Sparse Core Ops, SparseCore 0:
  9.8 59.1 all-gather.2

commit v8 on v7

--- a/solution.py
+++ b/solution.py
@@ -25,6 +25,7 @@
     downc_ref,
     out_ref,
     img_ref,
+    gath,
     fronts,
     fwd_buf,
     bwd_buf,
@@ -39,8 +40,12 @@
     hrecv,
     rsend,
     rrecv,
+    gsend,
+    grecv,
+    own_sem,
     *,
     n,
+    nv,
     nd,
     dc,
     per_block,
@@ -64,7 +69,7 @@
         (has_above, (h + 1, v, d)),
         (has_up, (h, v, d - 1)),
         (has_dn, (h, v, d + 1)),
-    ]
+    ] + [(v != p, (h, p, d)) for p in range(nv)]
     count = 0
     for cond, peer in peers:
         count = count + cond.astype(jnp.int32)
@@ -124,6 +129,25 @@
             device_id=(h, v, d + 1),
             device_id_type=MESH,
         )
+
+    def gather_copy(p, slot):
+        return pltpu.make_async_remote_copy(
+            src_ref=dir_ref,
+            dst_ref=gath.at[pl.ds(slot * blocks, blocks)],
+            send_sem=gsend.at[p],
+            recv_sem=grecv.at[slot],
+            device_id=(h, p, d),
+            device_id_type=MESH,
+        )
+
+    for p in range(nv):
+
+        @pl.when(v != p)
+        def _():
+            gather_copy(p, v).start()
+
+    own_copy = pltpu.make_async_copy(dir_ref, gath.at[pl.ds(v * blocks, blocks)], own_sem.at[0])
+    own_copy.start()
 
     @pl.when(has_below)
     def _():
@@ -266,9 +290,19 @@
         for a in range(rims):
             rim_copy(a).wait_send()
 
+    for p in range(nv):
+
+        @pl.when(v != p)
+        def _():
+            gather_copy(p, p).wait_recv()
+            gather_copy(p, v).wait_send()
+
+    own_copy.wait()
+
 
 def sweep(resid_l, dir_l, diag_l, lower_l, upper_l, pivot_l, downc_l, dc):
     n = lax.axis_size("elev")
+    nv = lax.axis_size("valley")
     nd = lax.axis_size("down")
     chunks, rows, width = resid_l.shape
     blocks = lower_l.shape[0]
@@ -277,13 +311,14 @@
     flops = 2 * (2 * chunks * rows + 4 * dir_l.shape[0] * dir_l.shape[1]) * width * width
     weight_bytes = 6 * lower_l.size * lower_l.dtype.itemsize
     return pl.pallas_call(
-        functools.partial(sweep_kernel, n=n, nd=nd, dc=dc, per_block=per_block),
+        functools.partial(sweep_kernel, n=n, nv=nv, nd=nd, dc=dc, per_block=per_block),
         out_shape=(
             jax.ShapeDtypeStruct(resid_l.shape, resid_l.dtype),
             jax.ShapeDtypeStruct(dir_l.shape, jnp.float32),
+            jax.ShapeDtypeStruct((nv * blocks,) + dir_l.shape[1:], dir_l.dtype),
         ),
         in_specs=[vmem] * 7,
-        out_specs=(vmem, vmem),
+        out_specs=(vmem, vmem, pl.BlockSpec(memory_space=pl.ANY)),
         scratch_shapes=[
             pltpu.VMEM(resid_l.shape, resid_l.dtype),
             pltpu.VMEM(resid_l.shape, resid_l.dtype),
@@ -299,6 +334,9 @@
             pltpu.SemaphoreType.DMA((2,)),
             pltpu.SemaphoreType.DMA((blocks // dc,)),
             pltpu.SemaphoreType.DMA((blocks // dc,)),
+            pltpu.SemaphoreType.DMA((nv,)),
+            pltpu.SemaphoreType.DMA((nv,)),
+            pltpu.SemaphoreType.DMA((1,)),
         ],
         compiler_params=pltpu.CompilerParams(collective_id=0, has_side_effects=True),
         cost_estimate=pl.CostEstimate(
@@ -362,7 +400,7 @@
     blocks = va * dc
     chunk_shape = (blocks * ROW_SPLIT, nr // ROW_SPLIT, bs)
     flat = (blocks, bs, bs)
-    solved, partial = sweep(
+    solved, partial, piece = sweep(
         resid[0].reshape(chunk_shape),
         direction[0].reshape(blocks, nr, bs),
         diag_blocks[0].reshape(flat),
@@ -373,11 +411,9 @@
         dc,
     )
 
-    current = direction[0]
-    piece = lax.all_gather(current, "valley", axis=0, tiled=True)
     image = add_partner(
         coupled_column,
-        piece.reshape((-1, nr, bs)),
+        piece,
         valley_coupling[0].reshape(flat),
         partial,
         dc,

time: 99.6 us -> 110 us (1.10)
  the two profiles are of different devices: /device:TPU:1 before, /device:TPU:30 now
where the time goes in v8:
time: 110 us; the launch traced here: 109 us
  Pallas kernels  107 us (97%)
  local copies, waits for them, and re-layouts  2.14 us (2%)
    pallas_call x1, Pallas kernels, sweep(): pl.pallas_call(functools.partial(sweep_kernel, n=n, nv=nv, nd=nd, dc=dc,...  102 us
    pallas_call x1, Pallas kernels, add_partner(): pl.pallas_call(functools.partial(partner_kernel, dc=dc), out_shape=jax.Sh...  4.96 us

profile of v8, /device:TPU:30, one launch (start us, length us, event | category | flops | bytes accessed | tf_op | source)
XLA Modules:
  0.0 109.4 jit_solution(12140402983090219112)
XLA Ops:
  0.6 1.3 %copy.11.col_ref = s32[1,4,2]{2,1,0:T(4,128)} copy(s32[1,4,2]{1,2,0:T(2,128)} %param.17) | data formatting | bytes 64 | tf_op args[8]
  2.0 101.6 %shard_map.104 = (bf16[16,64,256]{2,1,0:T(8,128)(2,1)}, f32[8,128,256]{2,1,0:T(8,128)}, bf16[64,128,256]{2,1,0:T(8,128)(2,1)}) custom-call(bf16[16,64,256]{2,1,0:T(8,128)(2,1)} %bitcast.17, bf16[8,128,256]{2,1,0:T(8,128)(2,1)} %bitcast.18, bf16[8,256,256]{2,1,0:T(8,128)(2,1)} %bitcast.10, bf16[8,256,256]{2,1,0:T(8,128)(2,1)} %bitcast.11, ...), custom_call_target="tpu_custom_call" | custom-call | flops 805306368 | bytes 9437184 | tf_op jit(solution)/shard_map/pallas_call | solution.py:313
  103.6 0.0 copy-start
  103.6 5.0 %shard_map.105 = f32[8,128,256]{2,1,0:T(8,128)} custom-call(s32[1,4,2]{2,1,0:T(4,128)} %copy.11.col_ref, bf16[64,128,256]{2,1,0:T(8,128)(2,1)} %get-tuple-element.6.piece_ref, bf16[8,256,256]{2,1,0:T(8,128)(2,1)} %bitcast.15, f32[8,128,256]{2,1,0:T(8,128)} %get-tuple-element.7.partial_ref), custom_call_target="tpu_custom_call" | custom-call | flops 134217728 | bytes 3670016 | tf_op jit(solution)/shard_map/pallas_call | solution.py:366
  108.6 0.0 copy-done
  108.6 0.8 copy.13
Async XLA Ops:
  103.6 5.0 %copy-start = (bf16[16,64,256]{2,1,0:T(8,128)(2,1)S(1)}, bf16[16,64,256]{2,1,0:T(8,128)(2,1)}, u32[]{:S(2)}) copy-start(bf16[16,64,256]{2,1,0:T(8,128)(2,1)} %get-tuple-element.5) | copy-start | bytes 1572868

commit v9 on v7

--- a/solution.py
+++ b/solution.py
@@ -307,44 +307,58 @@
     )(resid_l, dir_l, diag_l, lower_l, upper_l, pivot_l, downc_l)
 
 
-def partner_kernel(col_ref, piece_ref, valc_ref, partial_ref, out_ref, held, sems, *, dc):
+def partner_kernel(
+    col_ref, piece_ref, valc_ref, partial_ref, solved_ref, out_ref, solved_out,
+    held, vbuf, pbuf, sbuf, sems, *, dc
+):
     blocks = held.shape[0]
+    solved_in = pltpu.make_async_copy(solved_ref, sbuf, sems.at[0])
+    solved_in.start()
     copies = []
     for b in range(blocks):
         col = col_ref[0, b // dc, b % dc]
-        copy = pltpu.make_async_copy(piece_ref.at[col * dc + b % dc], held.at[b], sems.at[b])
-        copy.start()
-        copies.append(copy)
+        trio = (
+            pltpu.make_async_copy(piece_ref.at[col * dc + b % dc], held.at[b], sems.at[1 + 3 * b]),
+            pltpu.make_async_copy(valc_ref.at[b], vbuf.at[b], sems.at[2 + 3 * b]),
+            pltpu.make_async_copy(partial_ref.at[b], pbuf.at[b], sems.at[3 + 3 * b]),
+        )
+        for copy in trio:
+            copy.start()
+        copies.append(trio)
+    solved_in.wait()
+    solved_back = pltpu.make_async_copy(sbuf, solved_out, sems.at[1 + 3 * blocks])
+    solved_back.start()
     for b in range(blocks):
-        copies[b].wait()
-        out_ref[b] = partial_ref[b] + jnp.dot(
-            held[b], valc_ref[b], preferred_element_type=jnp.float32
-        )
-
-
-def add_partner(cols, piece, valc, partial, dc):
+        for copy in copies[b]:
+            copy.wait()
+        out_ref[b] = pbuf[b] + jnp.dot(held[b], vbuf[b], preferred_element_type=jnp.float32)
+    solved_back.wait()
+
+
+def add_partner(cols, piece, valc, partial, solved, dc):
     blocks, rows, width = partial.shape
-    vmem = pl.BlockSpec(memory_space=pltpu.VMEM)
+    hbm = pl.BlockSpec(memory_space=pl.ANY)
     return pl.pallas_call(
         functools.partial(partner_kernel, dc=dc),
-        out_shape=jax.ShapeDtypeStruct(partial.shape, partial.dtype),
-        in_specs=[
-            pl.BlockSpec(memory_space=pltpu.SMEM),
-            pl.BlockSpec(memory_space=pl.ANY),
-            vmem,
-            vmem,
-        ],
-        out_specs=vmem,
+        out_shape=(
+            jax.ShapeDtypeStruct(partial.shape, partial.dtype),
+            jax.ShapeDtypeStruct(solved.shape, solved.dtype),
+        ),
+        in_specs=[pl.BlockSpec(memory_space=pltpu.SMEM), hbm, hbm, hbm, hbm],
+        out_specs=(pl.BlockSpec(memory_space=pltpu.VMEM), hbm),
         scratch_shapes=[
             pltpu.VMEM((blocks, rows, width), piece.dtype),
-            pltpu.SemaphoreType.DMA((blocks,)),
+            pltpu.VMEM(valc.shape, valc.dtype),
+            pltpu.VMEM(partial.shape, partial.dtype),
+            pltpu.VMEM(solved.shape, solved.dtype),
+            pltpu.SemaphoreType.DMA((2 + 3 * blocks,)),
         ],
         cost_estimate=pl.CostEstimate(
             flops=2 * blocks * rows * width * width,
-            bytes_accessed=blocks * (rows * width * 10 + width * width * 2),
+            bytes_accessed=blocks * (rows * width * 10 + width * width * 2) + 4 * solved.size,
             transcendentals=0,
         ),
-    )(cols, piece, valc, partial)
+    )(cols, piece, valc, partial, solved)
 
 
 def local(
@@ -375,11 +389,12 @@
 
     current = direction[0]
     piece = lax.all_gather(current, "valley", axis=0, tiled=True)
-    image = add_partner(
+    image, solved = add_partner(
         coupled_column,
         piece.reshape((-1, nr, bs)),
         valley_coupling[0].reshape(flat),
         partial,
+        solved,
         dc,
     )
     return (solved.reshape(resid.shape), image.reshape(resid.shape))

time: 99.6 us -> 99 us (level)
  no operation moved by 1% of the time
where the time goes in v9:
time: 99 us; the launch traced here: 98.8 us
  Pallas kernels  82.7 us (84%)
  between operations  14.1 us (14%)
  local copies, waits for them, and re-layouts  1.35 us (1%)
    pallas_call x1, Pallas kernels, sweep(): pl.pallas_call(functools.partial(sweep_kernel, n=n, nd=nd, dc=dc, per_blo...  78.2 us
    pallas_call x1, Pallas kernels, add_partner(): pl.pallas_call(functools.partial(partner_kernel, dc=dc), out_shape=(jax.S...  4.49 us
  transfers between devices with their start and end apart: 1, of which 0 were waited for; matrix products, arithmetic and copies ran while one was open for 1% of the time, Pallas kernels for 79%

profile of v9, /device:TPU:1, one launch (start us, length us, event | category | flops | bytes accessed | tf_op | source)
XLA Modules:
  0.0 98.8 jit_solution(17786090219566545553)
XLA Ops:
  7.2 0.0 all-gather.3.cloned.1.call-start
  7.2 0.7 all-gather.3.cloned.1.call-update
  7.9 1.3 %copy.13.col_ref = s32[1,4,2]{2,1,0:T(4,128)} copy(s32[1,4,2]{1,2,0:T(2,128)} %param.17) | data formatting | bytes 64 | tf_op args[8]
  9.2 78.2 %shard_map.104 = (bf16[16,64,256]{2,1,0:T(8,128)(2,1)}, f32[8,128,256]{2,1,0:T(8,128)}) custom-call(bf16[16,64,256]{2,1,0:T(8,128)(2,1)} %bitcast.21, bf16[8,128,256]{2,1,0:T(8,128)(2,1)} %bitcast.14, bf16[8,256,256]{2,1,0:T(8,128)(2,1)} %bitcast.16, bf16[8,256,256]{2,1,0:T(8,128)(2,1)} %bitcast.17, bf16[8,256,256]{2,1,0:T(8,128)(2,1)} %bitcast.18, ...), custom_call_target="tpu_custom_call" | custom-call | flops 805306368 | bytes 9437184 | tf_op jit(solution)/shard_map/pallas_call | solution.py:279
  87.4 0.0 all-gather.3.cloned.1.call-done
  87.5 4.5 %shard_map.105 = (f32[8,128,256]{2,1,0:T(8,128)}, bf16[16,64,256]{2,1,0:T(8,128)(2,1)}) custom-call(s32[1,4,2]{2,1,0:T(4,128)} %copy.13.col_ref, bf16[64,128,256]{2,1,0:T(8,128)(2,1)} %bitcast.12, bf16[8,256,256]{2,1,0:T(8,128)(2,1)} %bitcast.15, f32[8,128,256]{2,1,0:T(8,128)} %get-tuple-element.6.partial_ref, bf16[16,64,256]{2,1,0:T(8,128)(2,1)} %get-tuple-element.7.solved_ref), custom_call_target="tpu_custom_call" | custom-call | flops 134217728 | bytes 4718592 | tf_op jit(solution)/shard_map/pallas_call | solution.py:341
Async XLA Ops:
  7.2 80.3 %all-gather.3.cloned.1.call-start = ((), (), s32[]{:S(2)}) async-start(), calls=%async_computation | async-start | bytes 4718592 | tf_op jit(solution)/shard_map/all_gather | solution.py:391
Sparse Core Ops, SparseCore 0:
  9.8 59.0 all-gather.2

commit v10 on v9

--- a/solution.py
+++ b/solution.py
@@ -16,13 +16,13 @@
 
 
 def sweep_kernel(
-    resid_ref,
-    dir_ref,
-    diag_ref,
-    lower_ref,
-    upper_ref,
-    pivot_ref,
-    downc_ref,
+    resid_hbm,
+    dir_hbm,
+    diag_hbm,
+    lower_hbm,
+    upper_hbm,
+    pivot_hbm,
+    downc_hbm,
     out_ref,
     img_ref,
     fronts,
@@ -39,6 +39,14 @@
     hrecv,
     rsend,
     rrecv,
+    resid_ref,
+    dir_ref,
+    diag_ref,
+    lower_ref,
+    upper_ref,
+    pivot_ref,
+    downc_ref,
+    load_sems,
     *,
     n,
     nd,
@@ -47,6 +55,22 @@
 ):
     f32 = jnp.float32
     bf16 = jnp.bfloat16
+    loads = [
+        pltpu.make_async_copy(src, dst, load_sems.at[i])
+        for i, (src, dst) in enumerate(
+            [
+                (resid_hbm, resid_ref),
+                (pivot_hbm, pivot_ref),
+                (lower_hbm, lower_ref),
+                (dir_hbm, dir_ref),
+                (upper_hbm, upper_ref),
+                (diag_hbm, diag_ref),
+                (downc_hbm, downc_ref),
+            ]
+        )
+    ]
+    for load in loads:
+        load.start()
     h = lax.axis_index("elev")
     v = lax.axis_index("valley")
     d = lax.axis_index("down")
@@ -125,15 +149,6 @@
             device_id_type=MESH,
         )
 
-    @pl.when(has_below)
-    def _():
-        halo_down().start()
-
-    @pl.when(has_dn)
-    def _():
-        for a in range(rims):
-            rim_copy(a).start()
-
     @pl.when(jnp.logical_not(has_below))
     def _():
         below_buf[...] = jnp.zeros(below_buf.shape, bf16)
@@ -179,7 +194,22 @@
 
         return carry
 
+    for load in loads[:3]:
+        load.wait()
+
     lax.fori_loop(0, chunks, fwd_body, 0)
+
+    for load in loads[3:]:
+        load.wait()
+
+    @pl.when(has_below)
+    def _():
+        halo_down().start()
+
+    @pl.when(has_dn)
+    def _():
+        for a in range(rims):
+            rim_copy(a).start()
 
     @pl.when(has_above)
     def _():
@@ -282,7 +312,7 @@
             jax.ShapeDtypeStruct(resid_l.shape, resid_l.dtype),
             jax.ShapeDtypeStruct(dir_l.shape, jnp.float32),
         ),
-        in_specs=[vmem] * 7,
+        in_specs=[pl.BlockSpec(memory_space=pl.ANY)] * 7,
         out_specs=(vmem, vmem),
         scratch_shapes=[
             pltpu.VMEM(resid_l.shape, resid_l.dtype),
@@ -299,6 +329,14 @@
             pltpu.SemaphoreType.DMA((2,)),
             pltpu.SemaphoreType.DMA((blocks // dc,)),
             pltpu.SemaphoreType.DMA((blocks // dc,)),
+            pltpu.VMEM(resid_l.shape, resid_l.dtype),
+            pltpu.VMEM(dir_l.shape, dir_l.dtype),
+            pltpu.VMEM(diag_l.shape, diag_l.dtype),
+            pltpu.VMEM(lower_l.shape, lower_l.dtype),
+            pltpu.VMEM(upper_l.shape, upper_l.dtype),
+            pltpu.VMEM(pivot_l.shape, pivot_l.dtype),
+            pltpu.VMEM(downc_l.shape, downc_l.dtype),
+            pltpu.SemaphoreType.DMA((7,)),
         ],
         compiler_params=pltpu.CompilerParams(collective_id=0, has_side_effects=True),
         cost_estimate=pl.CostEstimate(

time: 99 us -> 102 us (1.030)
  Pallas kernels: 82.7 us -> 86.1 us
    pallas_call x1, Pallas kernels: 78.2 us -> 81.5 us  [sweep(): pl.pallas_call(functools.partial(sweep_kernel, n=n, nd=nd, dc=dc, per_blo...]
  transfers between devices with their start and end apart: 1 -> 1, of which waited for: 0 -> 0; matrix products, arithmetic and copies ran while one was open for 1% -> 1% of each run, Pallas kernels for 79% -> 80%
where the time goes in v10:
time: 102 us
  Pallas kernels  86.1 us (84%)
  between operations  14.1 us (14%)
  local copies, waits for them, and re-layouts  1.35 us (1%)
    pallas_call x1, Pallas kernels, sweep(): pl.pallas_call(functools.partial(sweep_kernel, n=n, nd=nd, dc=dc, per_blo...  81.5 us
    pallas_call x1, Pallas kernels, add_partner(): pl.pallas_call(functools.partial(partner_kernel, dc=dc), out_shape=(jax.S...  4.56 us
  transfers between devices with their start and end apart: 1, of which 0 were waited for; matrix products, arithmetic and copies ran while one was open for 1% of the time, Pallas kernels for 80%

profile of v10, /device:TPU:1, one launch (start us, length us, event | category | flops | bytes accessed | tf_op | source)
XLA Modules:
  0.0 102.2 jit_solution(14263185298382342769)
XLA Ops:
  7.2 0.0 all-gather.3.cloned.1.call-start
  7.2 0.7 all-gather.3.cloned.1.call-update
  7.9 1.3 %copy.13.col_ref = s32[1,4,2]{2,1,0:T(4,128)} copy(s32[1,4,2]{1,2,0:T(2,128)} %param.17) | data formatting | bytes 64 | tf_op args[8]
  9.2 81.5 %shard_map.104 = (bf16[16,64,256]{2,1,0:T(8,128)(2,1)}, f32[8,128,256]{2,1,0:T(8,128)}) custom-call(bf16[16,64,256]{2,1,0:T(8,128)(2,1)} %bitcast.21, bf16[8,128,256]{2,1,0:T(8,128)(2,1)} %bitcast.14, bf16[8,256,256]{2,1,0:T(8,128)(2,1)} %bitcast.16, bf16[8,256,256]{2,1,0:T(8,128)(2,1)} %bitcast.17, bf16[8,256,256]{2,1,0:T(8,128)(2,1)} %bitcast.18, ...), custom_call_target="tpu_custom_call" | custom-call | flops 805306368 | bytes 9437184 | tf_op jit(solution)/shard_map/pallas_call | solution.py:309
  90.8 0.0 all-gather.3.cloned.1.call-done
  90.8 4.6 %shard_map.105 = (f32[8,128,256]{2,1,0:T(8,128)}, bf16[16,64,256]{2,1,0:T(8,128)(2,1)}) custom-call(s32[1,4,2]{2,1,0:T(4,128)} %copy.13.col_ref, bf16[64,128,256]{2,1,0:T(8,128)(2,1)} %bitcast.12, bf16[8,256,256]{2,1,0:T(8,128)(2,1)} %bitcast.15, f32[8,128,256]{2,1,0:T(8,128)} %get-tuple-element.6.partial_ref, bf16[16,64,256]{2,1,0:T(8,128)(2,1)} %get-tuple-element.7.solved_ref), custom_call_target="tpu_custom_call" | custom-call | flops 134217728 | bytes 4718592 | tf_op jit(solution)/shard_map/pallas_call | solution.py:379
Async XLA Ops:
  7.2 83.6 %all-gather.3.cloned.1.call-start = ((), (), s32[]{:S(2)}) async-start(), calls=%async_computation | async-start | bytes 4718592 | tf_op jit(solution)/shard_map/all_gather | solution.py:429
Sparse Core Ops, SparseCore 0:
  9.8 58.9 all-gather.2

commit v11 on v10

--- a/solution.py
+++ b/solution.py
@@ -59,10 +59,10 @@
         pltpu.make_async_copy(src, dst, load_sems.at[i])
         for i, (src, dst) in enumerate(
             [
+                (dir_hbm, dir_ref),
                 (resid_hbm, resid_ref),
                 (pivot_hbm, pivot_ref),
                 (lower_hbm, lower_ref),
-                (dir_hbm, dir_ref),
                 (upper_hbm, upper_ref),
                 (diag_hbm, diag_ref),
                 (downc_hbm, downc_ref),
@@ -194,13 +194,7 @@
 
         return carry
 
-    for load in loads[:3]:
-        load.wait()
-
-    lax.fori_loop(0, chunks, fwd_body, 0)
-
-    for load in loads[3:]:
-        load.wait()
+    loads[0].wait()
 
     @pl.when(has_below)
     def _():
@@ -210,6 +204,14 @@
     def _():
         for a in range(rims):
             rim_copy(a).start()
+
+    for load in loads[1:4]:
+        load.wait()
+
+    lax.fori_loop(0, chunks, fwd_body, 0)
+
+    for load in loads[4:]:
+        load.wait()
 
     @pl.when(has_above)
     def _():

time: 102 us -> 97.1 us (0.952)
  Pallas kernels: 86.1 us -> 80.8 us
    pallas_call x1, Pallas kernels: 81.5 us -> 76.3 us  [sweep(): pl.pallas_call(functools.partial(sweep_kernel, n=n, nd=nd, dc=dc, per_blo...]
  transfers between devices with their start and end apart: 1 -> 1, of which waited for: 0 -> 0; matrix products, arithmetic and copies ran while one was open for 1% -> 1% of each run, Pallas kernels for 80% -> 79%
where the time goes in v11:
time: 97.1 us; the launch traced here: 97 us
  Pallas kernels  80.8 us (83%)
  between operations  14.1 us (15%)
  local copies, waits for them, and re-layouts  1.35 us (1%)
    pallas_call x1, Pallas kernels, sweep(): pl.pallas_call(functools.partial(sweep_kernel, n=n, nd=nd, dc=dc, per_blo...  76.3 us
    pallas_call x1, Pallas kernels, add_partner(): pl.pallas_call(functools.partial(partner_kernel, dc=dc), out_shape=(jax.S...  4.49 us
  transfers between devices with their start and end apart: 1, of which 0 were waited for; matrix products, arithmetic and copies ran while one was open for 1% of the time, Pallas kernels for 79%

profile of v11, /device:TPU:1, one launch (start us, length us, event | category | flops | bytes accessed | tf_op | source)
XLA Modules:
  0.0 97.0 jit_solution(2524896918147960019)
XLA Ops:
  7.2 0.0 all-gather.3.cloned.1.call-start
  7.2 0.7 all-gather.3.cloned.1.call-update
  7.9 1.3 %copy.13.col_ref = s32[1,4,2]{2,1,0:T(4,128)} copy(s32[1,4,2]{1,2,0:T(2,128)} %param.17) | data formatting | bytes 64 | tf_op args[8]
  9.2 76.3 %shard_map.104 = (bf16[16,64,256]{2,1,0:T(8,128)(2,1)}, f32[8,128,256]{2,1,0:T(8,128)}) custom-call(bf16[16,64,256]{2,1,0:T(8,128)(2,1)} %bitcast.21, bf16[8,128,256]{2,1,0:T(8,128)(2,1)} %bitcast.14, bf16[8,256,256]{2,1,0:T(8,128)(2,1)} %bitcast.16, bf16[8,256,256]{2,1,0:T(8,128)(2,1)} %bitcast.17, bf16[8,256,256]{2,1,0:T(8,128)(2,1)} %bitcast.18, ...), custom_call_target="tpu_custom_call" | custom-call | flops 805306368 | bytes 9437184 | tf_op jit(solution)/shard_map/pallas_call | solution.py:311
  85.6 0.0 all-gather.3.cloned.1.call-done
  85.6 4.5 %shard_map.105 = (f32[8,128,256]{2,1,0:T(8,128)}, bf16[16,64,256]{2,1,0:T(8,128)(2,1)}) custom-call(s32[1,4,2]{2,1,0:T(4,128)} %copy.13.col_ref, bf16[64,128,256]{2,1,0:T(8,128)(2,1)} %bitcast.12, bf16[8,256,256]{2,1,0:T(8,128)(2,1)} %bitcast.15, f32[8,128,256]{2,1,0:T(8,128)} %get-tuple-element.6.partial_ref, bf16[16,64,256]{2,1,0:T(8,128)(2,1)} %get-tuple-element.7.solved_ref), custom_call_target="tpu_custom_call" | custom-call | flops 134217728 | bytes 4718592 | tf_op jit(solution)/shard_map/pallas_call | solution.py:381
Async XLA Ops:
  7.2 78.4 %all-gather.3.cloned.1.call-start = ((), (), s32[]{:S(2)}) async-start(), calls=%async_computation | async-start | bytes 4718592 | tf_op jit(solution)/shard_map/all_gather | solution.py:431
Sparse Core Ops, SparseCore 0:
  9.8 58.9 all-gather.2

commit v12 on v11

--- a/solution.py
+++ b/solution.py
@@ -9,6 +9,7 @@
 
 MESH = pl.DeviceIdType.MESH
 ROW_SPLIT = 2
+LAG = 3
 
 
 def apply_blocks(vectors, blocks):
@@ -162,6 +163,10 @@
         rim_buf[...] = jnp.zeros(rim_buf.shape, bf16)
 
     def fwd_body(g, carry):
+        fwd_step(g)
+        return carry
+
+    def fwd_step(g):
         blk = g // per_block
 
         @pl.when(has_below)
@@ -192,8 +197,6 @@
         def _():
             bwd_copy(g, fronts).start()
 
-        return carry
-
     loads[0].wait()
 
     @pl.when(has_below)
@@ -208,10 +211,49 @@
     for load in loads[1:4]:
         load.wait()
 
-    lax.fori_loop(0, chunks, fwd_body, 0)
-
-    for load in loads[4:]:
-        load.wait()
+    def bwd_body(g, carry):
+        bwd_step(g)
+        return carry
+
+    def bwd_step(g):
+        blk = g // per_block
+
+        @pl.when(has_above)
+        def _():
+            bwd_copy(g, out_ref).wait_recv()
+            carried = jnp.dot(bwd_buf[g], upper_ref[blk], preferred_element_type=f32).astype(bf16)
+            out_ref[g] = (
+                fronts[g].astype(f32) - jnp.dot(carried, pivot_ref[blk], preferred_element_type=f32)
+            ).astype(bf16)
+
+            @pl.when(has_below)
+            def _():
+                bwd_copy(g, out_ref).start()
+
+    is_turn = h == n - 2
+
+    def turn_body(i, carry):
+        @pl.when(i < chunks)
+        def _():
+            fwd_step(i)
+
+        @pl.when(i >= LAG)
+        def _():
+            bwd_step(i - LAG)
+
+        return carry
+
+    @pl.when(is_turn)
+    def _():
+        for load in loads[4:]:
+            load.wait()
+        lax.fori_loop(0, chunks + LAG, turn_body, 0)
+
+    @pl.when(jnp.logical_not(is_turn))
+    def _():
+        lax.fori_loop(0, chunks, fwd_body, 0)
+        for load in loads[4:]:
+            load.wait()
 
     @pl.when(has_above)
     def _():
@@ -249,24 +291,9 @@
     def _():
         image()
 
-    def bwd_body(g, carry):
-        blk = g // per_block
-
-        @pl.when(has_above)
-        def _():
-            bwd_copy(g, out_ref).wait_recv()
-            carried = jnp.dot(bwd_buf[g], upper_ref[blk], preferred_element_type=f32).astype(bf16)
-            out_ref[g] = (
-                fronts[g].astype(f32) - jnp.dot(carried, pivot_ref[blk], preferred_element_type=f32)
-            ).astype(bf16)
-
-            @pl.when(has_below)
-            def _():
-                bwd_copy(g, out_ref).start()
-
-        return carry
-
-    lax.fori_loop(0, chunks, bwd_body, 0)
+    @pl.when(jnp.logical_not(is_turn))
+    def _():
+        lax.fori_loop(0, chunks, bwd_body, 0)
 
     @pl.when(jnp.logical_not(early))
     def _():

time: 97.1 us -> 98.1 us (1.010)
  Pallas kernels: 80.8 us -> 81.8 us
where the time goes in v12:
time: 98.1 us; the launch traced here: 98 us
  Pallas kernels  81.8 us (83%)
  between operations  14.1 us (14%)
  local copies, waits for them, and re-layouts  1.35 us (1%)
    pallas_call x1, Pallas kernels, sweep(): pl.pallas_call(functools.partial(sweep_kernel, n=n, nd=nd, dc=dc, per_blo...  77.3 us
    pallas_call x1, Pallas kernels, add_partner(): pl.pallas_call(functools.partial(partner_kernel, dc=dc), out_shape=(jax.S...  4.52 us
  transfers between devices with their start and end apart: 1, of which 0 were waited for; matrix products, arithmetic and copies ran while one was open for 1% of the time, Pallas kernels for 79%

profile of v12, /device:TPU:1, one launch (start us, length us, event | category | flops | bytes accessed | tf_op | source)
XLA Modules:
  0.0 98.0 jit_solution(11835577737283453240)
XLA Ops:
  7.2 0.0 all-gather.3.cloned.1.call-start
  7.2 0.7 all-gather.3.cloned.1.call-update
  7.9 1.3 %copy.13.col_ref = s32[1,4,2]{2,1,0:T(4,128)} copy(s32[1,4,2]{1,2,0:T(2,128)} %param.17) | data formatting | bytes 64 | tf_op args[8]
  9.2 77.3 %shard_map.104 = (bf16[16,64,256]{2,1,0:T(8,128)(2,1)}, f32[8,128,256]{2,1,0:T(8,128)}) custom-call(bf16[16,64,256]{2,1,0:T(8,128)(2,1)} %bitcast.21, bf16[8,128,256]{2,1,0:T(8,128)(2,1)} %bitcast.14, bf16[8,256,256]{2,1,0:T(8,128)(2,1)} %bitcast.16, bf16[8,256,256]{2,1,0:T(8,128)(2,1)} %bitcast.17, bf16[8,256,256]{2,1,0:T(8,128)(2,1)} %bitcast.18, ...), custom_call_target="tpu_custom_call" | custom-call | flops 805306368 | bytes 9437184 | tf_op jit(solution)/shard_map/pallas_call | solution.py:338
  86.6 0.0 all-gather.3.cloned.1.call-done
  86.6 4.5 %shard_map.105 = (f32[8,128,256]{2,1,0:T(8,128)}, bf16[16,64,256]{2,1,0:T(8,128)(2,1)}) custom-call(s32[1,4,2]{2,1,0:T(4,128)} %copy.13.col_ref, bf16[64,128,256]{2,1,0:T(8,128)(2,1)} %bitcast.12, bf16[8,256,256]{2,1,0:T(8,128)(2,1)} %bitcast.15, f32[8,128,256]{2,1,0:T(8,128)} %get-tuple-element.6.partial_ref, bf16[16,64,256]{2,1,0:T(8,128)(2,1)} %get-tuple-element.7.solved_ref), custom_call_target="tpu_custom_call" | custom-call | flops 134217728 | bytes 4718592 | tf_op jit(solution)/shard_map/pallas_call | solution.py:408
Async XLA Ops:
  7.2 79.4 %all-gather.3.cloned.1.call-start = ((), (), s32[]{:S(2)}) async-start(), calls=%async_computation | async-start | bytes 4718592 | tf_op jit(solution)/shard_map/all_gather | solution.py:458
Sparse Core Ops, SparseCore 0:
  9.8 58.9 all-gather.2

commit v13 on v11

--- a/solution.py
+++ b/solution.py
@@ -195,15 +195,19 @@
         return carry
 
     loads[0].wait()
-
-    @pl.when(has_below)
-    def _():
-        halo_down().start()
-
-    @pl.when(has_dn)
-    def _():
-        for a in range(rims):
-            rim_copy(a).start()
+    send_early = h >= n // 2
+
+    def send_halos(when):
+        @pl.when(jnp.logical_and(has_below, when))
+        def _():
+            halo_down().start()
+
+        @pl.when(jnp.logical_and(has_dn, when))
+        def _():
+            for a in range(rims):
+                rim_copy(a).start()
+
+    send_halos(send_early)
 
     for load in loads[1:4]:
         load.wait()
@@ -212,6 +216,8 @@
 
     for load in loads[4:]:
         load.wait()
+
+    send_halos(jnp.logical_not(send_early))
 
     @pl.when(has_above)
     def _():

time: 97.1 us -> 97.2 us (level)
  no operation moved by 1% of the time
where the time goes in v13:
time: 97.2 us
  Pallas kernels  81 us (83%)
  between operations  14.1 us (15%)
  local copies, waits for them, and re-layouts  1.35 us (1%)
    pallas_call x1, Pallas kernels, sweep(): pl.pallas_call(functools.partial(sweep_kernel, n=n, nd=nd, dc=dc, per_blo...  76.4 us
    pallas_call x1, Pallas kernels, add_partner(): pl.pallas_call(functools.partial(partner_kernel, dc=dc), out_shape=(jax.S...  4.64 us
  transfers between devices with their start and end apart: 1, of which 0 were waited for; matrix products, arithmetic and copies ran while one was open for 1% of the time, Pallas kernels for 79%

profile of v13, /device:TPU:1, one launch (start us, length us, event | category | flops | bytes accessed | tf_op | source)
XLA Modules:
  0.0 97.2 jit_solution(3513085103566694366)
XLA Ops:
  7.2 0.0 all-gather.3.cloned.1.call-start
  7.2 0.7 all-gather.3.cloned.1.call-update
  7.9 1.3 %copy.13.col_ref = s32[1,4,2]{2,1,0:T(4,128)} copy(s32[1,4,2]{1,2,0:T(2,128)} %param.17) | data formatting | bytes 64 | tf_op args[8]
  9.2 76.4 %shard_map.104 = (bf16[16,64,256]{2,1,0:T(8,128)(2,1)}, f32[8,128,256]{2,1,0:T(8,128)}) custom-call(bf16[16,64,256]{2,1,0:T(8,128)(2,1)} %bitcast.21, bf16[8,128,256]{2,1,0:T(8,128)(2,1)} %bitcast.14, bf16[8,256,256]{2,1,0:T(8,128)(2,1)} %bitcast.16, bf16[8,256,256]{2,1,0:T(8,128)(2,1)} %bitcast.17, bf16[8,256,256]{2,1,0:T(8,128)(2,1)} %bitcast.18, ...), custom_call_target="tpu_custom_call" | custom-call | flops 805306368 | bytes 9437184 | tf_op jit(solution)/shard_map/pallas_call | solution.py:317
  85.6 0.0 all-gather.3.cloned.1.call-done
  85.7 4.6 %shard_map.105 = (f32[8,128,256]{2,1,0:T(8,128)}, bf16[16,64,256]{2,1,0:T(8,128)(2,1)}) custom-call(s32[1,4,2]{2,1,0:T(4,128)} %copy.13.col_ref, bf16[64,128,256]{2,1,0:T(8,128)(2,1)} %bitcast.12, bf16[8,256,256]{2,1,0:T(8,128)(2,1)} %bitcast.15, f32[8,128,256]{2,1,0:T(8,128)} %get-tuple-element.6.partial_ref, bf16[16,64,256]{2,1,0:T(8,128)(2,1)} %get-tuple-element.7.solved_ref), custom_call_target="tpu_custom_call" | custom-call | flops 134217728 | bytes 4718592 | tf_op jit(solution)/shard_map/pallas_call | solution.py:387
Async XLA Ops:
  7.2 78.5 %all-gather.3.cloned.1.call-start = ((), (), s32[]{:S(2)}) async-start(), calls=%async_computation | async-start | bytes 4718592 | tf_op jit(solution)/shard_map/all_gather | solution.py:437
Sparse Core Ops, SparseCore 0:
  9.8 58.9 all-gather.2

commit v14 on v13

--- a/solution.py
+++ b/solution.py
@@ -208,6 +208,11 @@
                 rim_copy(a).start()
 
     send_halos(send_early)
+    up_early = h >= n // 4
+
+    @pl.when(jnp.logical_and(has_above, up_early))
+    def _():
+        halo_up().start()
 
     for load in loads[1:4]:
         load.wait()
@@ -219,7 +224,7 @@
 
     send_halos(jnp.logical_not(send_early))
 
-    @pl.when(has_above)
+    @pl.when(jnp.logical_and(has_above, jnp.logical_not(up_early)))
     def _():
         halo_up().start()
 

time: 97.2 us -> 97.1 us (level)
  no operation moved by 1% of the time
where the time goes in v14:
time: 97.1 us; the launch traced here: 97 us
  Pallas kernels  80.9 us (83%)
  between operations  14.1 us (15%)
  local copies, waits for them, and re-layouts  1.35 us (1%)
    pallas_call x1, Pallas kernels, sweep(): pl.pallas_call(functools.partial(sweep_kernel, n=n, nd=nd, dc=dc, per_blo...  76.4 us
    pallas_call x1, Pallas kernels, add_partner(): pl.pallas_call(functools.partial(partner_kernel, dc=dc), out_shape=(jax.S...  4.5 us
  transfers between devices with their start and end apart: 1, of which 0 were waited for; matrix products, arithmetic and copies ran while one was open for 1% of the time, Pallas kernels for 79%

profile of v14, /device:TPU:1, one launch (start us, length us, event | category | flops | bytes accessed | tf_op | source)
XLA Modules:
  0.0 97.0 jit_solution(7431587017470631918)
XLA Ops:
  7.2 0.0 all-gather.3.cloned.1.call-start
  7.2 0.7 all-gather.3.cloned.1.call-update
  7.9 1.3 %copy.13.col_ref = s32[1,4,2]{2,1,0:T(4,128)} copy(s32[1,4,2]{1,2,0:T(2,128)} %param.17) | data formatting | bytes 64 | tf_op args[8]
  9.2 76.4 %shard_map.104 = (bf16[16,64,256]{2,1,0:T(8,128)(2,1)}, f32[8,128,256]{2,1,0:T(8,128)}) custom-call(bf16[16,64,256]{2,1,0:T(8,128)(2,1)} %bitcast.21, bf16[8,128,256]{2,1,0:T(8,128)(2,1)} %bitcast.14, bf16[8,256,256]{2,1,0:T(8,128)(2,1)} %bitcast.16, bf16[8,256,256]{2,1,0:T(8,128)(2,1)} %bitcast.17, bf16[8,256,256]{2,1,0:T(8,128)(2,1)} %bitcast.18, ...), custom_call_target="tpu_custom_call" | custom-call | flops 805306368 | bytes 9437184 | tf_op jit(solution)/shard_map/pallas_call | solution.py:322
  85.6 0.0 all-gather.3.cloned.1.call-done
  85.6 4.5 %shard_map.105 = (f32[8,128,256]{2,1,0:T(8,128)}, bf16[16,64,256]{2,1,0:T(8,128)(2,1)}) custom-call(s32[1,4,2]{2,1,0:T(4,128)} %copy.13.col_ref, bf16[64,128,256]{2,1,0:T(8,128)(2,1)} %bitcast.12, bf16[8,256,256]{2,1,0:T(8,128)(2,1)} %bitcast.15, f32[8,128,256]{2,1,0:T(8,128)} %get-tuple-element.6.partial_ref, bf16[16,64,256]{2,1,0:T(8,128)(2,1)} %get-tuple-element.7.solved_ref), custom_call_target="tpu_custom_call" | custom-call | flops 134217728 | bytes 4718592 | tf_op jit(solution)/shard_map/pallas_call | solution.py:392
Async XLA Ops:
  7.2 78.5 %all-gather.3.cloned.1.call-start = ((), (), s32[]{:S(2)}) async-start(), calls=%async_computation | async-start | bytes 4718592 | tf_op jit(solution)/shard_map/all_gather | solution.py:442
Sparse Core Ops, SparseCore 0:
  9.8 58.9 all-gather.2

commit v15 on v13

--- a/solution.py
+++ b/solution.py
@@ -359,7 +359,6 @@
 ):
     blocks = held.shape[0]
     solved_in = pltpu.make_async_copy(solved_ref, sbuf, sems.at[0])
-    solved_in.start()
     copies = []
     for b in range(blocks):
         col = col_ref[0, b // dc, b % dc]
@@ -371,13 +370,14 @@
         for copy in trio:
             copy.start()
         copies.append(trio)
-    solved_in.wait()
-    solved_back = pltpu.make_async_copy(sbuf, solved_out, sems.at[1 + 3 * blocks])
-    solved_back.start()
+    solved_in.start()
     for b in range(blocks):
         for copy in copies[b]:
             copy.wait()
         out_ref[b] = pbuf[b] + jnp.dot(held[b], vbuf[b], preferred_element_type=jnp.float32)
+    solved_in.wait()
+    solved_back = pltpu.make_async_copy(sbuf, solved_out, sems.at[1 + 3 * blocks])
+    solved_back.start()
     solved_back.wait()
 
 

time: 97.2 us -> 97.8 us (level)
  transfers between devices with their start and end apart: 1 -> 1, of which waited for: 0 -> 0; matrix products, arithmetic and copies ran while one was open for 1% -> 1% of each run, Pallas kernels for 79% -> 78%
where the time goes in v15:
time: 97.8 us; the launch traced here: 97.7 us
  Pallas kernels  81.5 us (83%)
  between operations  14.1 us (14%)
  local copies, waits for them, and re-layouts  1.35 us (1%)
    pallas_call x1, Pallas kernels, sweep(): pl.pallas_call(functools.partial(sweep_kernel, n=n, nd=nd, dc=dc, per_blo...  76.4 us
    pallas_call x1, Pallas kernels, add_partner(): pl.pallas_call(functools.partial(partner_kernel, dc=dc), out_shape=(jax.S...  5.17 us
  transfers between devices with their start and end apart: 1, of which 0 were waited for; matrix products, arithmetic and copies ran while one was open for 1% of the time, Pallas kernels for 78%

profile of v15, /device:TPU:1, one launch (start us, length us, event | category | flops | bytes accessed | tf_op | source)
XLA Modules:
  0.0 97.7 jit_solution(10525432902240513655)
XLA Ops:
  7.2 0.0 all-gather.3.cloned.1.call-start
  7.2 0.7 all-gather.3.cloned.1.call-update
  7.9 1.3 %copy.13.col_ref = s32[1,4,2]{2,1,0:T(4,128)} copy(s32[1,4,2]{1,2,0:T(2,128)} %param.17) | data formatting | bytes 64 | tf_op args[8]
  9.2 76.4 %shard_map.104 = (bf16[16,64,256]{2,1,0:T(8,128)(2,1)}, f32[8,128,256]{2,1,0:T(8,128)}) custom-call(bf16[16,64,256]{2,1,0:T(8,128)(2,1)} %bitcast.21, bf16[8,128,256]{2,1,0:T(8,128)(2,1)} %bitcast.14, bf16[8,256,256]{2,1,0:T(8,128)(2,1)} %bitcast.16, bf16[8,256,256]{2,1,0:T(8,128)(2,1)} %bitcast.17, bf16[8,256,256]{2,1,0:T(8,128)(2,1)} %bitcast.18, ...), custom_call_target="tpu_custom_call" | custom-call | flops 805306368 | bytes 9437184 | tf_op jit(solution)/shard_map/pallas_call | solution.py:317
  85.6 0.0 all-gather.3.cloned.1.call-done
  85.7 5.2 %shard_map.105 = (f32[8,128,256]{2,1,0:T(8,128)}, bf16[16,64,256]{2,1,0:T(8,128)(2,1)}) custom-call(s32[1,4,2]{2,1,0:T(4,128)} %copy.13.col_ref, bf16[64,128,256]{2,1,0:T(8,128)(2,1)} %bitcast.12, bf16[8,256,256]{2,1,0:T(8,128)(2,1)} %bitcast.15, f32[8,128,256]{2,1,0:T(8,128)} %get-tuple-element.6.partial_ref, bf16[16,64,256]{2,1,0:T(8,128)(2,1)} %get-tuple-element.7.solved_ref), custom_call_target="tpu_custom_call" | custom-call | flops 134217728 | bytes 4718592 | tf_op jit(solution)/shard_map/pallas_call | solution.py:387
Async XLA Ops:
  7.2 78.5 %all-gather.3.cloned.1.call-start = ((), (), s32[]{:S(2)}) async-start(), calls=%async_computation | async-start | bytes 4718592 | tf_op jit(solution)/shard_map/all_gather | solution.py:437
Sparse Core Ops, SparseCore 0:
  9.8 58.9 all-gather.2

commit v16 on v13

--- a/solution.py
+++ b/solution.py
@@ -59,10 +59,10 @@
         pltpu.make_async_copy(src, dst, load_sems.at[i])
         for i, (src, dst) in enumerate(
             [
-                (dir_hbm, dir_ref),
                 (resid_hbm, resid_ref),
                 (pivot_hbm, pivot_ref),
                 (lower_hbm, lower_ref),
+                (dir_hbm, dir_ref),
                 (upper_hbm, upper_ref),
                 (diag_hbm, diag_ref),
                 (downc_hbm, downc_ref),
@@ -195,7 +195,12 @@
         return carry
 
     loads[0].wait()
+    loads[1].wait()
     send_early = h >= n // 2
+
+    @pl.when(send_early)
+    def _():
+        loads[3].wait()
 
     def send_halos(when):
         @pl.when(jnp.logical_and(has_below, when))
@@ -209,10 +214,19 @@
 
     send_halos(send_early)
 
-    for load in loads[1:4]:
-        load.wait()
+    @pl.when(has_below)
+    def _():
+        loads[2].wait()
 
     lax.fori_loop(0, chunks, fwd_body, 0)
+
+    @pl.when(jnp.logical_not(has_below))
+    def _():
+        loads[2].wait()
+
+    @pl.when(jnp.logical_not(send_early))
+    def _():
+        loads[3].wait()
 
     for load in loads[4:]:
         load.wait()

time: 97.2 us -> 96.7 us (level)
  no operation moved by 1% of the time
where the time goes in v16:
time: 96.7 us; the launch traced here: 96.5 us
  Pallas kernels  80.4 us (83%)
  between operations  14.1 us (15%)
  local copies, waits for them, and re-layouts  1.35 us (1%)
    pallas_call x1, Pallas kernels, sweep(): pl.pallas_call(functools.partial(sweep_kernel, n=n, nd=nd, dc=dc, per_blo...  75.9 us
    pallas_call x1, Pallas kernels, add_partner(): pl.pallas_call(functools.partial(partner_kernel, dc=dc), out_shape=(jax.S...  4.49 us
  transfers between devices with their start and end apart: 1, of which 0 were waited for; matrix products, arithmetic and copies ran while one was open for 1% of the time, Pallas kernels for 79%

profile of v16, /device:TPU:1, one launch (start us, length us, event | category | flops | bytes accessed | tf_op | source)
XLA Modules:
  0.0 96.5 jit_solution(4977611947755947951)
XLA Ops:
  7.2 0.0 all-gather.3.cloned.1.call-start
  7.2 0.7 all-gather.3.cloned.1.call-update
  7.9 1.3 %copy.13.col_ref = s32[1,4,2]{2,1,0:T(4,128)} copy(s32[1,4,2]{1,2,0:T(2,128)} %param.17) | data formatting | bytes 64 | tf_op args[8]
  9.2 75.9 %shard_map.104 = (bf16[16,64,256]{2,1,0:T(8,128)(2,1)}, f32[8,128,256]{2,1,0:T(8,128)}) custom-call(bf16[16,64,256]{2,1,0:T(8,128)(2,1)} %bitcast.21, bf16[8,128,256]{2,1,0:T(8,128)(2,1)} %bitcast.14, bf16[8,256,256]{2,1,0:T(8,128)(2,1)} %bitcast.16, bf16[8,256,256]{2,1,0:T(8,128)(2,1)} %bitcast.17, bf16[8,256,256]{2,1,0:T(8,128)(2,1)} %bitcast.18, ...), custom_call_target="tpu_custom_call" | custom-call | flops 805306368 | bytes 9437184 | tf_op jit(solution)/shard_map/pallas_call | solution.py:331
  85.2 0.0 all-gather.3.cloned.1.call-done
  85.2 4.5 %shard_map.105 = (f32[8,128,256]{2,1,0:T(8,128)}, bf16[16,64,256]{2,1,0:T(8,128)(2,1)}) custom-call(s32[1,4,2]{2,1,0:T(4,128)} %copy.13.col_ref, bf16[64,128,256]{2,1,0:T(8,128)(2,1)} %bitcast.12, bf16[8,256,256]{2,1,0:T(8,128)(2,1)} %bitcast.15, f32[8,128,256]{2,1,0:T(8,128)} %get-tuple-element.6.partial_ref, bf16[16,64,256]{2,1,0:T(8,128)(2,1)} %get-tuple-element.7.solved_ref), custom_call_target="tpu_custom_call" | custom-call | flops 134217728 | bytes 4718592 | tf_op jit(solution)/shard_map/pallas_call | solution.py:401
Async XLA Ops:
  7.2 78.0 %all-gather.3.cloned.1.call-start = ((), (), s32[]{:S(2)}) async-start(), calls=%async_computation | async-start | bytes 4718592 | tf_op jit(solution)/shard_map/all_gather | solution.py:451
Sparse Core Ops, SparseCore 0:
  9.8 58.9 all-gather.2
